TPU v7x, 32 devices: a whole 2x2x4 slice. The times are simulated.
32 devices in a mesh: dp: 4 (over x, core), fsdp: 8 (over z, y).
Axes of the slice: x: 2, y: 2, z: 4, core: 2. Of those that a mesh axis runs over, the one named last changes fastest.
Arguments:
- inputs: bfloat16 [128, 280, 768], P(('dp', 'fsdp')), may hold values from -6 to 6
- patch_count: int32 [128], P(('dp', 'fsdp')), may hold values from 100 to 240
- cotangent: bfloat16 [128, 280, 768], P(('dp', 'fsdp')), may hold values from -6 to 6
- first_gain: bfloat16 [768], P('fsdp'), may hold values from 0.5 to 1.5
- first_shift: bfloat16 [768], P('fsdp'), may hold values from -1.796875 to 1.796875
- triple_weight: bfloat16 [768, 2304], P('fsdp'), may hold values from -0.21875 to 0.21875
- head_bias: bfloat16 [1536], P('fsdp'), may hold values from -1.796875 to 1.796875
- output_weight: bfloat16 [768, 768], P('fsdp'), may hold values from -0.875 to 0.875
- output_bias: bfloat16 [768], P('fsdp'), may hold values from -1.796875 to 1.796875
- second_gain: bfloat16 [768], P('fsdp'), may hold values from 0.5 to 1.5
- second_shift: bfloat16 [768], P('fsdp'), may hold values from -1.796875 to 1.796875
- expand_weight: bfloat16 [768, 3072], P('fsdp'), may hold values from -0.21875 to 0.21875
- expand_bias: bfloat16 [3072], P('fsdp'), may hold values from -1.796875 to 1.796875
- reduce_weight: bfloat16 [3072, 768], P('fsdp'), may hold values from -0.109375 to 0.109375
- reduce_bias: bfloat16 [768], P('fsdp'), may hold values from -1.796875 to 1.796875
Outputs:
- layer_output: bfloat16 [128, 280, 768], P(('dp', 'fsdp'))
- input_gradient: bfloat16 [128, 280, 768], P(('dp', 'fsdp'))
- first_gain_gradient: float32 [768], P('fsdp')
- first_shift_gradient: float32 [768], P('fsdp')
- triple_gradient: float32 [768, 2304], P('fsdp')
- head_bias_gradient: float32 [1536], P('fsdp')
- output_weight_gradient: float32 [768, 768], P('fsdp')
- output_bias_gradient: float32 [768], P('fsdp')
- second_gain_gradient: float32 [768], P('fsdp')
- second_shift_gradient: float32 [768], P('fsdp')
- expand_weight_gradient: float32 [768, 3072], P('fsdp')
- expand_bias_gradient: float32 [3072], P('fsdp')
- reduce_weight_gradient: float32 [3072, 768], P('fsdp')
- reduce_bias_gradient: float32 [768], P('fsdp')
Inputs may be any that keep to these rules, and one draw needn't show every extreme that they name: Rows 40 + patch_count to 279 of a pair are padding.
All inputs are finite; a program needn't handle non-finite values.
Results may differ from a plain program's by a relative error of at most 0.018.
Values may be sent and summed in bfloat16 or wider, within the bound.
A program may use at most 192 MiB of HBM per device.

v0:
```python
import jax
import jax.numpy as jnp
from jax import lax
from jax.sharding import PartitionSpec as P

HEADS = 12
HEAD_DIM = 64
TEXT = 40


NORM_EPSILON = 1e-06


def layer_norm(values, gain, shift):
    centred = values - jnp.mean(values, axis=-1, keepdims=True)
    variance = jnp.mean(centred * centred, axis=-1, keepdims=True)
    return centred * lax.rsqrt(variance + NORM_EPSILON) * gain + shift


def project_rows(left, right):
    return jnp.einsum("psd,de->pse", left, right, preferred_element_type=jnp.float32)


def back_rows(left, right):
    return jnp.einsum("pse,de->psd", left, right, preferred_element_type=jnp.float32)


def outer_rows(left, right):
    return jnp.einsum("psd,pse->de", left, right, preferred_element_type=jnp.float32)


def row_total(values):
    return jnp.sum(values.astype(jnp.float32), axis=(0, 1))


def shards(
    inputs,
    patch_count,
    cotangent,
    first_gain,
    first_shift,
    triple_weight,
    head_bias,
    output_weight,
    output_bias,
    second_gain,
    second_shift,
    expand_weight,
    expand_bias,
    reduce_weight,
    reduce_bias,
):
    gathered = (
        lax.all_gather(first_gain, "fsdp", axis=0, tiled=True),
        lax.all_gather(first_shift, "fsdp", axis=0, tiled=True),
        lax.all_gather(triple_weight, "fsdp", axis=0, tiled=True),
        lax.all_gather(head_bias, "fsdp", axis=0, tiled=True),
        lax.all_gather(output_weight, "fsdp", axis=0, tiled=True),
        lax.all_gather(output_bias, "fsdp", axis=0, tiled=True),
        lax.all_gather(second_gain, "fsdp", axis=0, tiled=True),
        lax.all_gather(second_shift, "fsdp", axis=0, tiled=True),
        lax.all_gather(expand_weight, "fsdp", axis=0, tiled=True),
        lax.all_gather(expand_bias, "fsdp", axis=0, tiled=True),
        lax.all_gather(reduce_weight, "fsdp", axis=0, tiled=True),
        lax.all_gather(reduce_bias, "fsdp", axis=0, tiled=True),
    )
    (
        gain_one,
        shift_one,
        triple,
        biases,
        project,
        project_bias,
        gain_two,
        shift_two,
        expand,
        expand_add,
        shrink,
        shrink_add,
    ) = gathered
    pairs, length, width = inputs.shape
    positions = lax.broadcasted_iota(jnp.int32, (pairs, length), 1)
    valid_rows = (positions < TEXT + patch_count[:, None]).astype(jnp.float32)
    key_mask = valid_rows[:, None, None, :] > 0
    score_scale = HEAD_DIM ** (-0.5)
    inputs_wide = inputs.astype(jnp.float32)
    hidden_one = layer_norm(
        inputs_wide, gain_one.astype(jnp.float32), shift_one.astype(jnp.float32)
    ).astype(jnp.bfloat16)
    biases_wide = biases.astype(jnp.float32)
    bias_row = jnp.concatenate(
        [biases_wide[:width], jnp.zeros((width,), jnp.float32), biases_wide[width:]]
    )
    triple_rows = (project_rows(hidden_one, triple) + bias_row).astype(jnp.bfloat16)
    query_rows = triple_rows[..., :width].reshape(pairs, length, HEADS, HEAD_DIM)
    key_rows = triple_rows[..., width : 2 * width].reshape(pairs, length, HEADS, HEAD_DIM)
    value_rows = triple_rows[..., 2 * width :].reshape(pairs, length, HEADS, HEAD_DIM)

    def scores_of(queries_in, keys_in):
        raw_scores = (
            jnp.einsum("pshd,pthd->phst", queries_in, keys_in, preferred_element_type=jnp.float32)
            * score_scale
        )
        return jnp.where(key_mask, raw_scores, -1e30)

    scores = scores_of(query_rows, key_rows)
    row_max = jnp.max(scores, axis=-1, keepdims=True)
    expo = jnp.exp(scores - row_max)
    expo_total = jnp.sum(expo, axis=-1, keepdims=True)
    probs = expo / expo_total
    row_lse = row_max + jnp.log(expo_total)
    context = jnp.einsum(
        "phst,pthd->pshd",
        probs.astype(jnp.bfloat16),
        value_rows,
        preferred_element_type=jnp.float32,
    )
    context = context.reshape(pairs, length, width).astype(jnp.bfloat16)
    middle = inputs_wide + project_rows(context, project) + project_bias.astype(jnp.float32)
    hidden_two = layer_norm(
        middle, gain_two.astype(jnp.float32), shift_two.astype(jnp.float32)
    ).astype(jnp.bfloat16)
    pre_act = project_rows(hidden_two, expand) + expand_add.astype(jnp.float32)
    activated = jax.nn.gelu(pre_act, approximate=False).astype(jnp.bfloat16)
    mixed = project_rows(activated, shrink) + shrink_add.astype(jnp.float32)
    layer_output = (valid_rows[..., None] * (middle + mixed)).astype(jnp.bfloat16)
    gain_one_back, triple_back, project_back, gain_two_back, expand_back, shrink_back = (
        lax.all_gather(first_gain, "fsdp", axis=0, tiled=True),
        lax.all_gather(triple_weight, "fsdp", axis=0, tiled=True),
        lax.all_gather(output_weight, "fsdp", axis=0, tiled=True),
        lax.all_gather(second_gain, "fsdp", axis=0, tiled=True),
        lax.all_gather(expand_weight, "fsdp", axis=0, tiled=True),
        lax.all_gather(reduce_weight, "fsdp", axis=0, tiled=True),
    )
    upstream = cotangent.astype(jnp.float32) * valid_rows[..., None]
    upstream_low = upstream.astype(jnp.bfloat16)
    shrink_add_grad = row_total(upstream_low)
    shrink_grad = outer_rows(activated, upstream_low)
    act_grad = back_rows(upstream_low, shrink_back)
    gelu_value, gelu_back = jax.vjp(lambda entry: jax.nn.gelu(entry, approximate=False), pre_act)
    pre_grad = gelu_back(act_grad)[0].astype(jnp.bfloat16)
    expand_add_grad = row_total(pre_grad)
    expand_grad = outer_rows(hidden_two, pre_grad)
    hidden_two_grad = back_rows(pre_grad, expand_back)
    zero_shift = jnp.zeros((width,), jnp.float32)
    norm_value, norm_back_two = jax.vjp(
        layer_norm, middle, gain_two_back.astype(jnp.float32), zero_shift
    )
    middle_part, gain_two_grad, shift_two_grad = norm_back_two(hidden_two_grad)
    middle_grad = upstream + middle_part
    branch_low = middle_grad.astype(jnp.bfloat16)
    project_bias_grad = row_total(branch_low)
    project_grad = outer_rows(context, branch_low)
    context_grad = (
        back_rows(branch_low, project_back)
        .astype(jnp.bfloat16)
        .reshape(pairs, length, HEADS, HEAD_DIM)
    )
    probs_again = jnp.exp(scores_of(query_rows, key_rows) - row_lse)
    value_grad = jnp.einsum(
        "phst,pshd->pthd",
        probs_again.astype(jnp.bfloat16),
        context_grad,
        preferred_element_type=jnp.float32,
    )
    probs_grad = jnp.einsum(
        "pshd,pthd->phst", context_grad, value_rows, preferred_element_type=jnp.float32
    )
    score_grad = (
        probs_again * (probs_grad - jnp.sum(probs_again * probs_grad, axis=-1, keepdims=True))
    ).astype(jnp.bfloat16)
    query_grad = (
        jnp.einsum("phst,pthd->pshd", score_grad, key_rows, preferred_element_type=jnp.float32)
        * score_scale
    )
    key_grad = (
        jnp.einsum("phst,pshd->pthd", score_grad, query_rows, preferred_element_type=jnp.float32)
        * score_scale
    )
    triple_grad_rows = jnp.concatenate(
        [
            query_grad.reshape(pairs, length, width),
            key_grad.reshape(pairs, length, width),
            value_grad.reshape(pairs, length, width),
        ],
        axis=-1,
    ).astype(jnp.bfloat16)
    bias_sums = row_total(triple_grad_rows)
    head_bias_grad = jnp.concatenate([bias_sums[:width], bias_sums[2 * width :]])
    triple_grad = outer_rows(hidden_one, triple_grad_rows)
    hidden_one_grad = back_rows(triple_grad_rows, triple_back)
    norm_again, norm_back_one = jax.vjp(
        layer_norm, inputs_wide, gain_one_back.astype(jnp.float32), zero_shift
    )
    input_part, gain_one_grad, shift_one_grad = norm_back_one(hidden_one_grad)
    input_gradient = (middle_grad + input_part).astype(jnp.bfloat16)
    shares = (
        lax.psum_scatter(
            gain_one_grad.astype(jnp.bfloat16), "fsdp", scatter_dimension=0, tiled=True
        ).astype(jnp.float32),
        lax.psum_scatter(
            shift_one_grad.astype(jnp.bfloat16), "fsdp", scatter_dimension=0, tiled=True
        ).astype(jnp.float32),
        lax.psum_scatter(
            triple_grad.astype(jnp.bfloat16), "fsdp", scatter_dimension=0, tiled=True
        ).astype(jnp.float32),
        lax.psum_scatter(
            head_bias_grad.astype(jnp.bfloat16), "fsdp", scatter_dimension=0, tiled=True
        ).astype(jnp.float32),
        lax.psum_scatter(
            project_grad.astype(jnp.bfloat16), "fsdp", scatter_dimension=0, tiled=True
        ).astype(jnp.float32),
        lax.psum_scatter(
            project_bias_grad.astype(jnp.bfloat16), "fsdp", scatter_dimension=0, tiled=True
        ).astype(jnp.float32),
        lax.psum_scatter(
            gain_two_grad.astype(jnp.bfloat16), "fsdp", scatter_dimension=0, tiled=True
        ).astype(jnp.float32),
        lax.psum_scatter(
            shift_two_grad.astype(jnp.bfloat16), "fsdp", scatter_dimension=0, tiled=True
        ).astype(jnp.float32),
        lax.psum_scatter(
            expand_grad.astype(jnp.bfloat16), "fsdp", scatter_dimension=0, tiled=True
        ).astype(jnp.float32),
        lax.psum_scatter(
            expand_add_grad.astype(jnp.bfloat16), "fsdp", scatter_dimension=0, tiled=True
        ).astype(jnp.float32),
        lax.psum_scatter(
            shrink_grad.astype(jnp.bfloat16), "fsdp", scatter_dimension=0, tiled=True
        ).astype(jnp.float32),
        lax.psum_scatter(
            shrink_add_grad.astype(jnp.bfloat16), "fsdp", scatter_dimension=0, tiled=True
        ).astype(jnp.float32),
    )
    totals = tuple(
        (
            lax.psum(shares[0].astype(jnp.bfloat16), "dp").astype(jnp.float32),
            lax.psum(shares[1].astype(jnp.bfloat16), "dp").astype(jnp.float32),
            lax.psum(shares[2].astype(jnp.bfloat16), "dp").astype(jnp.float32),
            lax.psum(shares[3].astype(jnp.bfloat16), "dp").astype(jnp.float32),
            lax.psum(shares[4].astype(jnp.bfloat16), "dp").astype(jnp.float32),
            lax.psum(shares[5].astype(jnp.bfloat16), "dp").astype(jnp.float32),
            lax.psum(shares[6].astype(jnp.bfloat16), "dp").astype(jnp.float32),
            lax.psum(shares[7].astype(jnp.bfloat16), "dp").astype(jnp.float32),
            lax.psum(shares[8].astype(jnp.bfloat16), "dp").astype(jnp.float32),
            lax.psum(shares[9].astype(jnp.bfloat16), "dp").astype(jnp.float32),
            lax.psum(shares[10].astype(jnp.bfloat16), "dp").astype(jnp.float32),
            lax.psum(shares[11].astype(jnp.bfloat16), "dp").astype(jnp.float32),
        )
    )
    return (layer_output, input_gradient) + tuple(totals)


def solution(mesh):
    in_specs = (
        P(("dp", "fsdp"), None, None),
        P(("dp", "fsdp")),
        P(("dp", "fsdp"), None, None),
        P("fsdp"),
        P("fsdp"),
        P("fsdp", None),
        P("fsdp"),
        P("fsdp", None),
        P("fsdp"),
        P("fsdp"),
        P("fsdp"),
        P("fsdp", None),
        P("fsdp"),
        P("fsdp", None),
        P("fsdp"),
    )
    out_specs = (
        P(("dp", "fsdp"), None, None),
        P(("dp", "fsdp"), None, None),
        P("fsdp"),
        P("fsdp"),
        P("fsdp", None),
        P("fsdp"),
        P("fsdp", None),
        P("fsdp"),
        P("fsdp"),
        P("fsdp"),
        P("fsdp", None),
        P("fsdp"),
        P("fsdp", None),
        P("fsdp"),
    )
    return jax.shard_map(shards, mesh=mesh, in_specs=in_specs, out_specs=out_specs, check_vma=False)
```

profile of v0, /device:TPU:1, one launch (start us, length us, event | category | flops | bytes accessed | tf_op | source)
XLA Modules:
  0.0 763.5 jit_solution(12241474160581128759)
XLA Ops:
  8.0 0.7 all-gather.8.cloned.1.call-update
  10.0 1.3 fusion.69
  13.3 0.7 reshape.198
  14.0 0.8 dynamic-update-slice.4
  14.8 0.8 dynamic-update-slice.5
  15.7 0.8 dynamic-update-slice.3
  16.5 0.8 dynamic-update-slice
  17.3 0.8 dynamic-update-slice.1
  18.2 0.8 dynamic-update-slice.2
  19.0 31.6 %all-reduce.16 = (bf16[1536]{0:T(1024)(128)(2,1)S(1)}, bf16[768]{0:T(1024)(128)(2,1)S(1)}, bf16[768]{0:T(1024)(128)(2,1)S(1)}, bf16[768]{0:T(1024)(128)(2,1)S(1)...) all-reduce(bf16[1536]{0:T(1024)(128)(2,1)S(1)} %dynamic-update-slic, ...), channel_id=1, replica_groups=mesh['dp'=4,'fsdp'=8] {'fsdp'}, use_global_device_ids=true, to_apply=%add.2 | all-reduce | flops 5376 | bytes 21504
  51.9 1.8 convert_reduce_fusion
  55.6 23.1 %all-gather = bf16[8,1,384]{2,1,0:T(2,128)(2,1)S(1)} all-gather(bf16[1,1,384]{2,1,0:T(2,128)(2,1)S(1)} %reshape.198), channel_id=1, replica_groups=mesh['dp'=4,'fsdp'=8] {'fsdp'}, dimensions={0}, use_global_device_ids=true | all-gather | bytes 6912 | tf_op jit(solution)/shard_map/all_gather | solution.py:63
  78.8 6.8 add_convert_fusion.1
  85.6 2.1 fusion.66
  87.7 2.5 copy.61
  90.2 2.9 copy.60
  93.1 4.4 copy.59
  97.4 11.1 %fusion.12 = (f32[4,12,280]{2,1,0:T(8,128)S(1)}, f32[4,12,280,280]{2,3,1,0:T(8,128)}) fusion(pred[4,280]{1,0:T(4,128)(4,1)S(1)} %get-tuple-element.67, bf16[4,280,12,64]{1,3,2,0:T(8,128)(2,1)S(1)} %bitcast.78, bf16[4,280,12,64]{1,3,2,0:T(8,128)(2,1)} %bitcast.80), kind=kOutput, calls=%fused_computation.35 | convolution fusion | flops 492965760 | bytes 18548320 | tf_op jit(solution)/shard_map/pshd,pthd->phst/dot_general | solution.py:101
  108.5 11.0 %fusion = f32[4,12,280]{2,1,0:T(8,128)S(1)} fusion(f32[4,12,280]{2,1,0:T(8,128)S(1)} %get-tuple-element.68, f32[4,12,280,280]{2,3,1,0:T(8,128)} %get-tuple-element.69, pred[4,280]{1,0:T(4,128)(4,1)S(1)} %get-tuple-element.67), kind=kLoop, calls=%fused_computation.7 | loop fusion | flops 15039360 | bytes 15161440 | tf_op jit(solution)/shard_map/reduce_sum | solution.py:109
  120.2 1.3 copy-done
  121.5 8.6 %fusion.38 = bf16[4,12,64,280]{3,2,1,0:T(8,128)(2,1)} fusion(bf16[4,280,12,64]{1,3,2,0:T(8,128)(2,1)} %bitcast.83, f32[4,12,280]{2,1,0:T(8,128)} %copy-done.16, f32[4,12,280]{2,1,0:T(8,128)S(1)} %get-tuple-element.68, f32[4,12,280,280]{2,3,1,0:T(8,128)S(1)} %copy-done, pred[4,280]{1,0:T(4,128)(4,1)S(1)} %get-tuple-element.67), kind=kOutput, calls=%fused_computation.79 | convolution fusion | flops 501365760 | bytes 18602080 | tf_op jit(solution)/shard_map/phst,pthd->pshd/dot_general | solution.py:112
  130.1 4.1 fusion.70
  134.3 1.7 copy-done.8
  137.2 62.9 %all-gather.10.cloned.1.call-done = bf16[768,3072]{1,0:T(8,128)(2,1)} async-done(((bf16[96,3072]{1,0:T(8,128)(2,1)}), bf16[768,3072]{1,0:T(8,128)(2,1)}) %all-gather.10.cloned.1.call-update) | async-done | bytes 4718608 | tf_op jit(solution)/shard_map/all_gather | solution.py:62
  200.0 14.3 %fusion.37 = (u8[280,3072]{1,0:T(8,128)(4,1)S(1)}, u8[280,3072]{1,0:T(8,128)(4,1)S(1)}, f32[4,280,3072]{2,1,0:T(8,128)S(1)}) fusion(f32[3072]{0:T(1024)S(1)} %bitcast.89, bf16[768,3072]{1,0:T(8,128)(2,1)} %all-gather.10.cloned.1.call-done, f32[4,280,768]{2,1,0:T(8,128)} %copy-done.8, f32[768]{0:T(1024)S(1)} %copy-done.38, ...), kind=kOutput, calls=%fused_computation.77 | convolution fusion | flops 5335572480 | bytes 23669504 | tf_op jit(solution)/shard_map/psd,de->pse/dot_general | solution.py:21
  214.4 4.9 copy-done.7
  219.3 32.8 %multiply_convert_fusion.1 = (bf16[4,280,3072]{2,1,0:T(8,128)(2,1)}, f32[4,280,3072]{2,1,0:T(8,128)}) fusion(f32[4,280,3072]{2,1,0:T(8,128)S(1)} %get-tuple-element.72, f32[3072]{0:T(1024)S(1)} %bitcast.90, u8[280,3072]{1,0:T(8,128)(4,1)S(1)} %get-tuple-element.15, u8[280,3072]{1,0:T(8,128)(4,1)S(1)} %get-tuple-element.14), kind=kLoop, calls=%fused_computation.16 | loop fusion | flops 244285440 | bytes 36139008 | tf_op jit(solution)/shard_map/convert_element_type | solution.py:124
  252.1 28.0 %all-gather.12.cloned.1.call-done = bf16[3072,768]{1,0:T(8,128)(2,1)} async-done(((bf16[384,768]{1,0:T(8,128)(2,1)}), bf16[3072,768]{1,0:T(8,128)(2,1)}) %all-gather.12.cloned.1.call-update) | async-done | bytes 4718608 | tf_op jit(solution)/shard_map/all_gather | solution.py:64
  280.1 18.9 %fusion.71 = (bf16[3072]{0:T(1024)(128)(2,1)}, bf16[4,280,3072]{2,1,0:T(8,128)(2,1)}) fusion(f32[4,280,3072]{2,1,0:T(8,128)} %get-tuple-element.55, bf16[3072,768]{1,0:T(8,128)(2,1)} %all-gather.12.cloned.1.call-done, bf16[4,280,768]{2,1,0:T(8,128)(2,1)} %param.17, f32[4,280]{1,0:T(4,128)} %get-tuple-element.66, f32[4,280,3072]{2,1,0:T(8,128)} %copy-done.7, ...), kind=kOutput, calls=%fused_computation.117 | convolution fusion | flops 5342450688 | bytes 40868224 | tf_op jit(solution)/shard_map/pse,de->psd/dot_general | solution.py:25
  299.0 10.7 %multiply_reduce_fusion.1 = (bf16[768]{0:T(1024)(128)(2,1)}, f32[4,280]{1,0:T(4,128)S(1)}, bf16[768]{0:T(1024)(128)(2,1)}, f32[4,280,768]{2,1,0:T(8,128)S(1)}) fusion(f32[4,280,768]{2,1,0:T(8,128)S(1)} %copy-done.9, f32[4,280]{1,0:T(4,128)} %copy-done.32, f32[4,280]{1,0:T(4,128)S(1)} %broadcast_multiply_fusion, f32[768]{0:T(1024)S(1)} %convert_element_type.198, ...), kind=kOutput, calls=%fused_computation.67 | convolution fusion | flops 5291701248 | bytes 18500736 | tf_op jit(solution)/shard_map/pse,de->psd/dot_general | solution.py:25
  309.7 1.3 fusion.64
  311.1 1.4 fusion.62
  312.6 1.2 copy-done.15
  313.7 2.7 bitcast_convert_fusion.3
  316.5 4.5 convolution_convert_fusion
  321.0 4.4 copy.64
  325.4 14.0 %fusion.39 = bf16[4,12,64,280]{3,2,1,0:T(8,128)(2,1)} fusion(bf16[4,280,12,64]{1,3,2,0:T(8,128)(2,1)} %bitcast.85, f32[4,12,280]{2,1,0:T(8,128)S(1)} %log_add_fusion, f32[4,12,280,280]{2,3,1,0:T(8,128)} %get-tuple-element.69, pred[4,280]{1,0:T(4,128)(4,1)S(1)} %get-tuple-element.67), kind=kOutput, calls=%fused_computation.80 | convolution fusion | flops 497602560 | bytes 18548320 | tf_op jit(solution)/shard_map/phst,pshd->pthd/dot_general | solution.py:160
  339.4 17.5 %multiply_reduce_fusion = (f32[4,12,280]{2,1,0:T(8,128)}, f32[4,12,280,280]{2,3,1,0:T(8,128)}) fusion(f32[4,12,280]{2,1,0:T(8,128)S(1)} %log_add_fusion, f32[4,12,280,280]{2,3,1,0:T(8,128)} %get-tuple-element.69, pred[4,280]{1,0:T(4,128)(4,1)S(1)} %get-tuple-element.67, bf16[4,280,12,64]{1,3,2,0:T(8,128)(2,1)} %bitcast.86, bf16[4,280,12,64]{1,3,2,0:T(8,128)(2,1)} %bitcast.84), kind=kOutput, calls=%fused_computation.1 | convolution fusion | flops 500492160 | bytes 33654880 | tf_op jit(solution)/shard_map/pshd,pthd->phst/dot_general | solution.py:166
  357.0 15.2 %multiply_convert_fusion = bf16[4,12,280,280]{2,3,1,0:T(8,128)(2,1)S(1)} fusion(f32[4,12,280,280]{2,3,1,0:T(8,128)} %get-tuple-element.75, f32[4,12,280]{2,1,0:T(8,128)} %get-tuple-element.74, f32[4,12,280]{2,1,0:T(8,128)S(1)} %log_add_fusion, f32[4,12,280,280]{2,3,1,0:T(8,128)} %get-tuple-element.69, pred[4,280]{1,0:T(4,128)(4,1)S(1)} %get-tuple-element.67), kind=kLoop, calls=%fused_computation | loop fusion | flops 22579200 | bytes 37740640 | tf_op jit(solution)/shard_map/convert_element_type | solution.py:171
  372.2 4.2 multiply_convert_fusion.3
  376.8 4.1 copy.70
  380.9 4.1 copy.68
  385.0 9.7 %multiply_convert_fusion.2 = bf16[4,12,64,280]{3,2,1,0:T(8,128)(2,1)} fusion(bf16[4,280,12,64]{1,3,2,0:T(8,128)(2,1)} %bitcast.79, bf16[4,12,280,280]{2,3,1,0:T(8,128)(2,1)} %copy-done.1), kind=kOutput, calls=%fused_computation.54 | convolution fusion | flops 483409920 | bytes 10967040 | tf_op jit(solution)/shard_map/phst,pshd->pthd/dot_general | solution.py:177
  394.7 4.1 copy.69
  398.8 9.9 %bitcast_convert_fusion.2 = bf16[768,2304]{1,0:T(8,128)(2,1)} fusion(bf16[4,280,768]{2,1,0:T(8,128)(2,1)} %param.15, f32[768]{0:T(1024)S(1)} %copy-done.41, f32[768]{0:T(1024)S(1)} %copy-done.31, f32[4,280]{1,0:T(4,128)S(1)} %copy-done.24, f32[4,280]{1,0:T(4,128)S(1)} %copy-done.18, bf16[4,280,768]{2,1,0:T(8,128)(2,1)} %copy.70, ...), kind=kOutput, calls=%fused_computation.36 | convolution fusion | flops 3986030592 | bytes 10435328 | tf_op jit(solution)/shard_map/psd,pse->de/dot_general | solution.py:29
  408.8 12.1 %bitcast_convert_fusion.1 = bf16[768,3072]{1,0:T(8,128)(2,1)} fusion(bf16[4,280,3072]{2,1,0:T(8,128)(2,1)} %get-tuple-element.78, f32[4,280,768]{2,1,0:T(8,128)} %copy-done.8, f32[768]{0:T(1024)S(1)} %copy-done.39, f32[768]{0:T(1024)S(1)} %convert_element_type.198, f32[4,280]{1,0:T(4,128)S(1)} %copy-done.34, f32[4,280]{1,0:T(4,128)S(1)} %broadcast_multiply_fusion), kind=kOutput, calls=%fused_computation.34 | convolution fusion | flops 5291483136 | bytes 15055616 | tf_op jit(solution)/shard_map/psd,pse->de/dot_general | solution.py:29
  421.6 10.7 %bitcast_convert_fusion = bf16[3072,768]{1,0:T(8,128)(2,1)} fusion(bf16[4,280,3072]{2,1,0:T(8,128)(2,1)} %get-tuple-element.54, bf16[4,280,768]{2,1,0:T(8,128)(2,1)} %param.17, f32[4,280]{1,0:T(4,128)S(1)} %copy-done.28), kind=kOutput, calls=%fused_computation.33 | convolution fusion | flops 5289762816 | bytes 13324672 | tf_op jit(solution)/shard_map/psd,pse->de/dot_general | solution.py:29
  434.7 4.4 fusion.60
  439.1 7.2 fusion.61
  446.4 1.7 fusion.31
  448.2 29.7 %all-reduce.15 = (bf16[768]{0:T(1024)(128)(2,1)S(1)}, bf16[768]{0:T(1024)(128)(2,1)}, bf16[768]{0:T(1024)(128)(2,1)}, bf16[1536]{0:T(1024)(128)(2,1)S(1)}, bf16[...) all-reduce(bf16[768]{0:T(1024)(128)(2,1)S(1)} %dynamic-update-slice, ...), channel_id=1, replica_groups=mesh['dp'=4,'fsdp'=8] {'fsdp'}, use_global_device_ids=true, to_apply=%add.6 | all-reduce | flops 9984 | bytes 39936
  477.9 0.8 dynamic-slice.8
  478.7 0.8 dynamic-slice.10
  479.4 0.8 dynamic-slice.14
  480.6 12.9 %all-reduce.17 = (bf16[96]{0:T(256)(128)(2,1)S(1)}, bf16[96]{0:T(256)(128)(2,1)S(1)}, bf16[192]{0:T(256)(128)(2,1)S(1)}, bf16[96]{0:T(256)(128)(2,1)S(1)}, bf16[...) all-reduce(bf16[96]{0:T(256)(128)(2,1)S(1)} %dynamic-slice.8, ...), channel_id=1, replica_groups=mesh['dp'=4,'fsdp'=8] {'dp'}, use_global_device_ids=true, to_apply=%region_13.14 | all-reduce | flops 1152 | bytes 4608 | tf_op jit(solution)/shard_map/psum | solution.py:237
  497.7 10.6 %multiply_convert_fusion.4 = bf16[4,280,768]{2,1,0:T(8,128)(2,1)} fusion(f32[4,280,768]{2,1,0:T(8,128)} %copy-done.8, bf16[4,280,3072]{2,1,0:T(8,128)(2,1)} %get-tuple-element.54, bf16[3072,768]{1,0:T(8,128)(2,1)} %all-gather.12.cloned.1.call-done, f32[768]{0:T(1024)S(1)} %convert_element_type.203, f32[4,280]{1,0:T(4,128)S(1)} %copy-done.28), kind=kOutput, calls=%fused_computation.73 | convolution fusion | flops 5288263680 | bytes 16768384 | tf_op jit(solution)/shard_map/psd,de->pse/dot_general | solution.py:21
  508.3 92.8 %reduce-scatter.9.cloned.1.call-done = bf16[96,3072]{1,0:T(8,128)(2,1)} async-done(((bf16[768,3072]{1,0:T(8,128)(2,1)}), bf16[96,3072]{1,0:T(8,128)(2,1)}) %reduce-scatter.9.cloned.1.call-update) | async-done | bytes 589840 | tf_op jit(solution)/shard_map/reduce_scatter | solution.py:222
  601.1 98.7 %reduce-scatter.11.cloned.1.call-done = bf16[384,768]{1,0:T(8,128)(2,1)} async-done(((bf16[3072,768]{1,0:T(8,128)(2,1)}), bf16[384,768]{1,0:T(8,128)(2,1)}) %reduce-scatter.11.cloned.1.call-update) | async-done | bytes 589840 | tf_op jit(solution)/shard_map/reduce_scatter | solution.py:228
  699.8 4.8 add_convert_fusion.2
  704.6 44.1 %all-reduce.21.cloned.1.call-done = (bf16[96,2304]{1,0:T(8,128)(2,1)}, bf16[96,768]{1,0:T(8,128)(2,1)}, bf16[96,3072]{1,0:T(8,128)(2,1)}, bf16[384,768]{1,0:T(8,128)(2,1)}) async-done(((bf16[96,2304]{1,0:T(8,128)(2,1)}, bf16[96,768]{1,0:T(8,128)(2,1)}, bf16[96,3072]{1,0:T(8,128)(2,1)}, bf16[384,768]{1,0:T(8,128)(2,1)}), (bf16[96,2304]{1,0:T(8,128)(2,1)}, bf16[96,768]{1,0:T(8,128)(2,1)}, ...) | async-done | bytes 1769488 | tf_op jit(solution)/shard_map/psum | solution.py:239
  748.7 1.6 convert_element_type.222
  750.4 2.0 convert_element_type.218
  752.4 2.2 convert_element_type.229
  754.5 2.2 convert_element_type.232
  (157 shorter events, 14.1 us)
Async XLA Ops:
  7.2 46.5 %copy-start.3 = (bf16[4,280,768]{2,1,0:T(8,128)(2,1)S(1)}, bf16[4,280,768]{2,1,0:T(8,128)(2,1)}, u32[]{:S(2)}) copy-start(bf16[4,280,768]{2,1,0:T(8,128)(2,1)} %param.15) | copy-start | bytes 5160964
  7.2 71.6 %all-gather.6.cloned.1.call-start = ((), (), s32[]{:S(2)}) async-start(), calls=%async_computation.4 | async-start | bytes 3981312 | tf_op jit(solution)/shard_map/all_gather | solution.py:56
  7.9 122.2 %all-gather.8.cloned.1.call-start = ((), (), s32[]{:S(2)}) async-start(), calls=%async_computation.5 | async-start | bytes 1327104 | tf_op jit(solution)/shard_map/all_gather | solution.py:58
  8.7 191.3 %all-gather.10.cloned.1.call-start = ((), (), s32[]{:S(2)}) async-start(), calls=%async_computation.6 | async-start | bytes 5308416 | tf_op jit(solution)/shard_map/all_gather | solution.py:62
  9.4 270.7 %all-gather.12.cloned.1.call-start = ((), (), s32[]{:S(2)}) async-start(), calls=%async_computation.7 | async-start | bytes 5308416 | tf_op jit(solution)/shard_map/all_gather | solution.py:64
  10.0 498.3 %reduce-scatter.7.cloned.1.call-start = ((), (), s32[]{:S(2)}) async-start(), calls=%async_computation.9 | async-start | bytes 1327104 | tf_op jit(solution)/shard_map/reduce_scatter | solution.py:210
  50.7 35.0 %copy-start.30 = (f32[768]{0:T(1024)}, f32[768]{0:T(1024)S(1)}, u32[]{:S(2)}) copy-start(f32[768]{0:T(1024)S(1)} %convert_element_type.188) | copy-start | bytes 9220
  50.7 35.0 %copy-start.40 = (f32[768]{0:T(1024)}, f32[768]{0:T(1024)S(1)}, u32[]{:S(2)}) copy-start(f32[768]{0:T(1024)S(1)} %convert_element_type.189) | copy-start | bytes 9220
  53.7 32.0 %copy-start.17 = (f32[4,280]{1,0:T(4,128)}, f32[4,280]{1,0:T(4,128)S(1)}, u32[]{:S(2)}) copy-start(f32[4,280]{1,0:T(4,128)S(1)} %broadcast_multiply_fusion.1) | copy-start | bytes 13444
  54.3 0.6 copy-start.19
  54.9 30.7 %copy-start.23 = (f32[4,280]{1,0:T(4,128)}, f32[4,280]{1,0:T(4,128)S(1)}, u32[]{:S(2)}) copy-start(f32[4,280]{1,0:T(4,128)S(1)} %fusion.54) | copy-start | bytes 13444
  78.7 135.7 %copy-start.29 = (f32[8,1,384]{2,1,0:T(1,128)}, f32[8,1,384]{2,1,0:T(1,128)S(1)}, u32[]{:S(2)}) copy-start(f32[8,1,384]{2,1,0:T(1,128)S(1)} %convert_element_type.234) | copy-start | bytes 36868
  93.1 15.5 %copy-start.2 = (bf16[4,280,768]{1,2,0:T(8,128)(2,1)}, bf16[4,280,768]{1,2,0:T(8,128)(2,1)S(1)}, u32[]{:S(2)}) copy-start(bf16[4,280,768]{1,2,0:T(8,128)(2,1)S(1)} %copy.60) | copy-start | bytes 5160964
  108.5 12.9 %copy-start = (f32[4,12,280,280]{2,3,1,0:T(8,128)S(1)}, f32[4,12,280,280]{2,3,1,0:T(8,128)}, u32[]{:S(2)}) copy-start(f32[4,12,280,280]{2,3,1,0:T(8,128)} %get-tuple-element.69) | copy-start | bytes 45158404
  119.6 0.6 copy-start.16
  121.5 8.6 %copy-start.4 = (bf16[4,280,768]{2,1,0:T(8,128)(2,1)S(1)}, bf16[4,280,768]{2,1,0:T(8,128)(2,1)}, u32[]{:S(2)}) copy-start(bf16[4,280,768]{2,1,0:T(8,128)(2,1)} %param.15) | copy-start | bytes 5160964
  121.5 8.6 %copy-start.42 = (f32[768]{0:T(1024)S(1)}, f32[768]{0:T(1024)}, u32[]{:S(2)}) copy-start(f32[768]{0:T(1024)} %convert_element_type.197) | copy-start | bytes 9220
  130.1 69.9 %copy-start.38 = (f32[768]{0:T(1024)S(1)}, f32[768]{0:T(1024)}, u32[]{:S(2)}) copy-start(f32[768]{0:T(1024)} %convert_element_type.199) | copy-start | bytes 9220
  134.2 1.8 copy-start.8
  136.5 0.6 copy-start.21
  137.2 77.2 %copy-start.32 = (f32[4,280]{1,0:T(4,128)}, f32[4,280]{1,0:T(4,128)S(1)}, u32[]{:S(2)}) copy-start(f32[4,280]{1,0:T(4,128)S(1)} %fusion.55) | copy-start | bytes 13444
  214.4 4.9 copy-start.7
  280.1 18.9 %copy-start.9 = (f32[4,280,768]{2,1,0:T(8,128)S(1)}, f32[4,280,768]{2,1,0:T(8,128)}, u32[]{:S(2)}) copy-start(f32[4,280,768]{2,1,0:T(8,128)} %copy-done.8) | copy-start | bytes 10321924
  299.0 10.7 %copy-start.22 = (f32[4,280]{1,0:T(4,128)S(1)}, f32[4,280]{1,0:T(4,128)}, u32[]{:S(2)}) copy-start(f32[4,280]{1,0:T(4,128)} %copy-done.21) | copy-start | bytes 13444
  299.0 10.7 %copy-start.10 = (f32[4,280,768]{2,1,0:T(8,128)S(1)}, f32[4,280,768]{2,1,0:T(8,128)}, u32[]{:S(2)}) copy-start(f32[4,280,768]{2,1,0:T(8,128)} %copy-done.8) | copy-start | bytes 10321924
  299.0 10.7 %copy-start.33 = (f32[4,280]{1,0:T(4,128)S(1)}, f32[4,280]{1,0:T(4,128)}, u32[]{:S(2)}) copy-start(f32[4,280]{1,0:T(4,128)} %copy-done.32) | copy-start | bytes 13444
  309.7 1.5 copy-start.12
  309.7 1.5 copy-start.27
  311.0 2.7 copy-start.46
  311.1 1.5 copy-start.25
  312.5 1.2 copy-start.15
  356.9 151.4 %reduce-scatter.5.cloned.1.call-start = ((), (), s32[]{:S(2)}) async-start(), calls=%async_computation.8 | async-start | bytes 3981312 | tf_op jit(solution)/shard_map/reduce_scatter | solution.py:204
  357.0 15.2 %copy-start.6 = (bf16[4,280,768]{1,2,0:T(8,128)(2,1)S(1)}, bf16[4,280,768]{1,2,0:T(8,128)(2,1)}, u32[]{:S(2)}) copy-start(bf16[4,280,768]{1,2,0:T(8,128)(2,1)} %copy.61) | copy-start | bytes 5160964
  372.2 4.7 copy-start.1
  385.0 13.8 %copy-start.18 = (f32[4,280]{1,0:T(4,128)S(1)}, f32[4,280]{1,0:T(4,128)}, u32[]{:S(2)}) copy-start(f32[4,280]{1,0:T(4,128)} %copy-done.17) | copy-start | bytes 13444
  385.0 13.8 %copy-start.24 = (f32[4,280]{1,0:T(4,128)S(1)}, f32[4,280]{1,0:T(4,128)}, u32[]{:S(2)}) copy-start(f32[4,280]{1,0:T(4,128)} %copy-done.23) | copy-start | bytes 13444
  385.0 13.8 %copy-start.31 = (f32[768]{0:T(1024)S(1)}, f32[768]{0:T(1024)}, u32[]{:S(2)}) copy-start(f32[768]{0:T(1024)} %copy-done.30) | copy-start | bytes 9220
  385.0 13.8 %copy-start.41 = (f32[768]{0:T(1024)S(1)}, f32[768]{0:T(1024)}, u32[]{:S(2)}) copy-start(f32[768]{0:T(1024)} %copy-done.40) | copy-start | bytes 9220
  398.8 10.0 %copy-start.34 = (f32[4,280]{1,0:T(4,128)S(1)}, f32[4,280]{1,0:T(4,128)}, u32[]{:S(2)}) copy-start(f32[4,280]{1,0:T(4,128)} %copy-done.32) | copy-start | bytes 13444
  398.8 10.0 %copy-start.39 = (f32[768]{0:T(1024)S(1)}, f32[768]{0:T(1024)}, u32[]{:S(2)}) copy-start(f32[768]{0:T(1024)} %convert_element_type.199) | copy-start | bytes 9220
  408.7 192.4 %reduce-scatter.9.cloned.1.call-start = ((), (), s32[]{:S(2)}) async-start(), calls=%async_computation.10 | async-start | bytes 5308416 | tf_op jit(solution)/shard_map/reduce_scatter | solution.py:222
  420.9 0.7 copy-start.28
  421.0 278.8 %reduce-scatter.11.cloned.1.call-start = ((), (), s32[]{:S(2)}) async-start(), calls=%async_computation.11 | async-start | bytes 5308416 | tf_op jit(solution)/shard_map/reduce_scatter | solution.py:228
  432.4 2.0 copy-start.45
  432.4 316.3 %all-reduce.21.cloned.1.call-start = ((), (), s32[]{:S(2)}) async-start(), calls=%async_computation.12 | async-start | bytes 3538944 | tf_op jit(solution)/shard_map/psum | solution.py:239
  434.6 4.5 copy-start.5
  434.6 4.5 copy-start.13
  434.6 4.5 copy-start.14
  439.1 7.3 copy-start.20
  446.4 1.8 copy-start.11
  446.4 1.8 copy-start.35
  446.4 1.8 copy-start.36
  446.4 1.8 copy-start.37
  446.4 1.8 copy-start.43
  446.4 1.8 copy-start.44
  497.7 202.1 %copy-start.26 = (f32[4,280]{1,0:T(4,128)S(1)}, f32[4,280]{1,0:T(4,128)}, u32[]{:S(2)}) copy-start(f32[4,280]{1,0:T(4,128)} %copy-done.25) | copy-start | bytes 13444
Sparse Core Ops, SparseCore 0:
  10.2 66.7 all-gather.5
  79.2 39.6 all-gather.7
  121.1 78.9 all-gather.9
  202.0 78.0 all-gather.11
  357.0 61.6 reduce-scatter.6
  422.2 80.1 reduce-scatter.4
  506.0 95.0 reduce-scatter.8
  604.8 94.9 reduce-scatter.10
  702.4 46.3 all-reduce.20
where the time goes:
time: 768 us; the launch traced here: 763 us
  waiting for transfers between devices  329 us (43%)
  matrix products  178 us (23%)
  blocking collectives  97.3 us (13%)
  other arithmetic  90.4 us (12%)
  local copies, waits for them, and re-layouts  50.5 us (7%)
  between operations  18 us (2%)
    reduce_scatter x1, waiting for transfers between devices, shards(): lax.psum_scatter(shrink_grad.astype(jnp.bfloat16), 'fsdp', scatter_dimens...  98.7 us
    reduce_scatter x1, waiting for transfers between devices, shards(): lax.psum_scatter(expand_grad.astype(jnp.bfloat16), 'fsdp', scatter_dimens...  92.8 us
    all_gather x1, waiting for transfers between devices, shards(): lax.all_gather(expand_weight, 'fsdp', axis=0, tiled=True)  62.9 us
    unnamed x2, blocking collectives  61.3 us
    psum x1, waiting for transfers between devices, shards(): lax.psum(shares[2].astype(jnp.bfloat16), 'dp').astype(jnp.float32)  44.1 us
    dot_general x4, matrix products, back_rows(): jnp.einsum('pse,de->psd', left, right, preferred_element_type=jnp.float32)  41.3 us
    dot_general x4, matrix products, project_rows(): jnp.einsum('psd,de->pse', left, right, preferred_element_type=jnp.float32)  35.9 us
    dot_general x4, matrix products, outer_rows(): jnp.einsum('psd,pse->de', left, right, preferred_element_type=jnp.float32)  35.5 us
  transfers between devices with their start and end apart: 9, of which 5 were waited for; matrix products, arithmetic and copies ran while one was open for 29% of the time, Pallas kernels for 0%

commit v1 on v0

--- a/solution.py
+++ b/solution.py
@@ -1,11 +1,488 @@
+import functools
+
 import jax
 import jax.numpy as jnp
 from jax import lax
+from jax.experimental import pallas as pl
+from jax.experimental.pallas import tpu as pltpu
 from jax.sharding import PartitionSpec as P
 
 HEADS = 12
 HEAD_DIM = 64
 TEXT = 40
+MESH = pl.DeviceIdType.MESH
+
+
+class Grid:
+    def __init__(self, fsdp, dp):
+        self.H = dp // 4
+        y_size = 1
+        while y_size * y_size * 8 <= fsdp:
+            y_size *= 2
+        self.F, self.Y, self.Z = fsdp, y_size, fsdp // y_size
+
+    def locate(self):
+        self.dp = lax.axis_index("dp")
+        self.f = lax.axis_index("fsdp")
+        self.c = lax.rem(self.dp, 2)
+        self.x = lax.rem(self.dp // 2, 2)
+        self.h = self.dp // 4
+        self.z = self.f // self.Y
+        self.y = lax.rem(self.f, self.Y)
+        return self
+
+    def core_peer(self):
+        return (self.dp + 1 - 2 * self.c, self.f)
+
+    def x_peer(self):
+        return (self.dp + 2 - 4 * self.x, self.f)
+
+    def far_index(self, dh):
+        return lax.rem(self.h + self.H + dh, self.H)
+
+    def far_peer(self, dh):
+        return (self.far_index(dh) * 4 + lax.rem(self.dp, 4), self.f)
+
+    def z_index(self, dz):
+        return lax.rem(self.z + self.Z + dz, self.Z)
+
+    def y_index(self, dy):
+        return lax.rem(self.y + self.Y + dy, self.Y)
+
+    def z_peer(self, dz):
+        return (self.dp, self.z_index(dz) * self.Y + self.y)
+
+    def y_peer(self, dy):
+        return (self.dp, self.z * self.Y + self.y_index(dy))
+
+    def source(self, dz, dy):
+        return self.z_index(-dz) * self.Y + self.y_index(-dy)
+
+    def greet(self):
+        barrier = pltpu.get_barrier_semaphore()
+        peers = [self.core_peer(), self.x_peer()]
+        peers += [self.z_peer(dz) for dz in range(1, self.Z)]
+        peers += [self.y_peer(dy) for dy in range(1, self.Y)]
+        peers += [self.far_peer(dh) for dh in range(1, self.H)]
+        for peer in peers:
+            pl.semaphore_signal(barrier, inc=1, device_id=peer, device_id_type=MESH)
+        pl.semaphore_wait(barrier, len(peers))
+
+
+def remote(src, dst, send, recv, peer):
+    return pltpu.make_async_remote_copy(
+        src_ref=src,
+        dst_ref=dst,
+        send_sem=send,
+        recv_sem=recv,
+        device_id=peer,
+        device_id_type=MESH,
+    )
+
+
+def lanes(start, width):
+    return pl.ds(pl.multiple_of(start, 128), width)
+
+
+class Gather:
+    def __init__(self, grid, src, dst, rows, col, width, send, recv):
+        self.g, self.src, self.dst, self.rows = grid, src, dst, rows
+        self.send, self.recv = send, recv
+        self.half, self.group = width // 2, width // 6
+        self.col = col
+        self.sent = []
+        g = grid
+        self.mine = lanes(col + g.c * self.half + g.x * self.group, 2 * self.group)
+        self.x_out = lanes(col + g.c * self.half + 2 * g.x * self.group, self.group)
+        self.x_in = lanes(col + g.c * self.half + 2 * (1 - g.x) * self.group, self.group)
+        self.core_out = lanes(col + g.c * self.half, self.half)
+        self.core_in = lanes(col + (1 - g.c) * self.half, self.half)
+        self.z_base, self.y_base = 0, g.Z - 1
+        self.x_base = self.y_base + g.Z * (g.Y - 1)
+        self.c_base = self.x_base + g.F - 1
+
+    @staticmethod
+    def count(grid):
+        return grid.Z - 1 + grid.Z * (grid.Y - 1) + 2 * (grid.F - 1)
+
+    def view(self, shard, columns):
+        return self.dst.at[shard, self.rows, columns]
+
+    def push(self, src, dst, index, peer):
+        copy = remote(src, dst, self.send.at[index], self.recv.at[index], peer)
+        copy.start()
+        self.sent.append(copy)
+
+    def arrive(self, view, index):
+        pltpu.make_async_copy(view, view, self.recv.at[index]).wait()
+
+    def pairs(self):
+        return [(dz, dy) for dy in range(self.g.Y) for dz in range(self.g.Z) if dz + dy > 0]
+
+    def slot(self, dz, dy):
+        return dz * self.g.Y + dy - 1
+
+    def begin(self):
+        g = self.g
+        own = self.src.at[self.rows, self.mine]
+        for dz in range(1, g.Z):
+            self.push(own, self.view(g.f, self.mine), self.z_base + dz - 1, g.z_peer(dz))
+        for dy in range(1, g.Y):
+            self.push(own, self.view(g.f, self.mine), self.y_base + dy - 1, g.y_peer(dy))
+
+    def over_y(self):
+        g = self.g
+        for dz in range(1, g.Z):
+            shard = g.source(dz, 0)
+            self.arrive(self.view(shard, self.mine), self.z_base + dz - 1)
+            for dy in range(1, g.Y):
+                self.push(
+                    self.view(shard, self.mine),
+                    self.view(shard, self.mine),
+                    self.y_base + dz * (g.Y - 1) + dy - 1,
+                    g.y_peer(dy),
+                )
+            self.over_x(dz, 0)
+
+    def over_x(self, dz, dy):
+        g = self.g
+        shard = g.source(dz, dy)
+        self.push(
+            self.view(shard, self.x_out),
+            self.view(shard, self.x_out),
+            self.x_base + self.slot(dz, dy),
+            g.x_peer(),
+        )
+
+    def finish_y(self):
+        g = self.g
+        for dz in range(g.Z):
+            for dy in range(1, g.Y):
+                shard = g.source(dz, dy)
+                self.arrive(self.view(shard, self.mine), self.y_base + dz * (g.Y - 1) + dy - 1)
+                self.over_x(dz, dy)
+
+    def over_core(self):
+        g = self.g
+        for dz, dy in self.pairs():
+            shard = g.source(dz, dy)
+            self.arrive(self.view(shard, self.x_in), self.x_base + self.slot(dz, dy))
+            self.push(
+                self.view(shard, self.core_out),
+                self.view(shard, self.core_out),
+                self.c_base + self.slot(dz, dy),
+                g.core_peer(),
+            )
+
+    def finish(self):
+        g = self.g
+        for dz, dy in self.pairs():
+            shard = g.source(dz, dy)
+            self.arrive(self.view(shard, self.core_in), self.c_base + self.slot(dz, dy))
+
+    def drain(self):
+        for copy in self.sent:
+            copy.wait_send()
+
+
+def gather_kernel(grid, pieces, *refs):
+    n = len(pieces)
+    count = refs_count(pieces)
+    sources, outs = refs[:count], refs[count : 2 * count]
+    send, recv, local = refs[2 * count :]
+    grid.locate()
+    owns = []
+    for index in range(count):
+        own = pltpu.make_async_copy(sources[index], outs[index].at[grid.f], local.at[index])
+        own.start()
+        owns.append(own)
+    grid.greet()
+    chunks = [
+        Gather(grid, sources[which], outs[which], pl.ds(row, rows), col, width, send.at[i], recv.at[i])
+        for i, (which, row, rows, col, width) in enumerate(pieces)
+    ]
+    for chunk in chunks:
+        chunk.begin()
+    for step in range(n + 2):
+        if step < n:
+            chunks[step].over_y()
+        if 0 <= step - 1 < n:
+            chunks[step - 1].finish_y()
+        if 0 <= step - 2 < n:
+            chunks[step - 2].over_core()
+    for chunk in chunks:
+        chunk.finish()
+    for chunk in chunks:
+        chunk.drain()
+    for own in owns:
+        own.wait()
+
+
+def refs_count(pieces):
+    return 1 + max(piece[0] for piece in pieces)
+
+
+def gather_all(fsdp, dp, arrays):
+    grid = Grid(fsdp, dp)
+    pieces = []
+    for which, array in enumerate(arrays):
+        rows, width = array.shape
+        if rows * width < 96 * 3072 * 96 // fsdp // 12 // 8 * 8 or which < 3:
+            pieces.append((which, 0, rows, 0, width))
+        elif width > 1536:
+            pieces.append((which, 0, rows, 0, width // 2))
+            pieces.append((which, 0, rows, width // 2, width // 2))
+        else:
+            pieces.append((which, 0, rows // 2, 0, width))
+            pieces.append((which, rows // 2, rows // 2, 0, width))
+    count = Gather.count(grid)
+    hbm = pl.BlockSpec(memory_space=pltpu.HBM)
+    return pl.pallas_call(
+        functools.partial(gather_kernel, grid, pieces),
+        out_shape=[jax.ShapeDtypeStruct((fsdp,) + a.shape, a.dtype) for a in arrays],
+        in_specs=[hbm] * len(arrays),
+        out_specs=[hbm] * len(arrays),
+        scratch_shapes=[
+            pltpu.SemaphoreType.DMA((len(pieces), count)),
+            pltpu.SemaphoreType.DMA((len(pieces), count)),
+            pltpu.SemaphoreType.DMA((len(arrays),)),
+        ],
+        compiler_params=pltpu.CompilerParams(collective_id=0, has_side_effects=True),
+        name="gather_weights",
+    )(*arrays)
+
+
+class Scatter:
+    def __init__(self, grid, src, out, rows, col, width, apart, bufs, send, recv, local):
+        g = self.g = grid
+        self.src, self.out, self.rows = src, out, rows
+        self.send, self.recv, self.local = send, recv, local
+        self.half, self.apart = width // 2, apart
+        self.shared = self.half - 2 * apart
+        self.core_keep = lanes(col + g.c * self.half, self.half)
+        self.core_give = lanes(col + (1 - g.c) * self.half, self.half)
+        self.x_keep = lanes(g.x * (apart + self.shared), apart)
+        self.x_give = lanes((1 - g.x) * (apart + self.shared), apart)
+        self.kept = lanes(g.x * apart, apart + self.shared)
+        self.out_keep, self.out_give = self.core_keep, self.core_give
+        self.near, self.core_in, self.x_in, self.y_in, self.z_sum, self.z_in, self.f_out, self.f_in, self.e_out, self.far = bufs
+        self.sent = []
+
+    @staticmethod
+    def buffers(grid, rows, width, apart):
+        half = width // 2
+        part = half - apart
+        bf = jnp.bfloat16
+        return [
+            pltpu.VMEM((grid.F, rows, half), bf),
+            pltpu.VMEM((grid.F, rows, half), bf),
+            pltpu.VMEM((grid.F, rows, apart), bf),
+            pltpu.VMEM((grid.Y, grid.Z, rows, part), bf),
+            pltpu.VMEM((grid.Z, rows, part), bf),
+            pltpu.VMEM((grid.Z, rows, part), bf),
+            pltpu.VMEM((rows, part), bf),
+            pltpu.VMEM((rows, part), bf),
+            pltpu.VMEM((2, rows, half), bf),
+            pltpu.VMEM((grid.H, rows, part), bf),
+        ]
+
+    @staticmethod
+    def count(grid):
+        return 4 + grid.Z * (grid.Y - 1) + grid.Z - 1 + grid.H - 1
+
+    def push(self, src, dst, index, peer):
+        copy = remote(src, dst, self.send.at[index], self.recv.at[index], peer)
+        copy.start()
+        self.sent.append(copy)
+
+    def arrive(self, view, index):
+        pltpu.make_async_copy(view, view, self.recv.at[index]).wait()
+
+    def begin(self):
+        self.own = pltpu.make_async_copy(self.src.at[:, self.rows, self.core_keep], self.near, self.local)
+        self.own.start()
+        self.push(self.src.at[:, self.rows, self.core_give], self.core_in, 0, self.g.core_peer())
+
+    def add(self, count, body):
+        def step(i, carry):
+            body(i)
+            return carry
+
+        lax.fori_loop(0, count, step, 0)
+
+    def over_x(self):
+        self.own.wait()
+        self.arrive(self.core_in, 0)
+
+        def body(i):
+            self.near[i] = plus(self.near[i], self.core_in[i])
+
+        self.add(self.g.F, body)
+        self.push(self.near.at[:, :, self.x_give], self.x_in, 1, self.g.x_peer())
+
+    def over_y(self):
+        g = self.g
+        self.arrive(self.x_in, 1)
+
+        def body(i):
+            self.near[i, :, self.x_keep] = plus(self.near[i, :, self.x_keep], self.x_in[i])
+
+        self.add(g.F, body)
+        for dz in range(g.Z):
+            for dy in range(1, g.Y):
+                self.push(
+                    self.near.at[dz * g.Y + g.y_index(dy), :, self.kept],
+                    self.y_in.at[dy, dz],
+                    4 + dz * (g.Y - 1) + dy - 1,
+                    g.y_peer(dy),
+                )
+
+    def over_z(self):
+        g = self.g
+        for dz in range(g.Z):
+            for dy in range(1, g.Y):
+                self.arrive(self.y_in.at[dy, dz], 4 + dz * (g.Y - 1) + dy - 1)
+
+        def body(i):
+            total = self.near[i * g.Y + g.y, :, self.kept].astype(jnp.float32)
+            for dy in range(1, g.Y):
+                total += self.y_in[dy, i].astype(jnp.float32)
+            self.z_sum[i] = total.astype(jnp.bfloat16)
+
+        self.add(g.Z, body)
+        for dz in range(1, g.Z):
+            self.push(
+                self.z_sum.at[g.z_index(dz)],
+                self.z_in.at[dz],
+                4 + g.Z * (g.Y - 1) + dz - 1,
+                g.z_peer(dz),
+            )
+
+    def over_pair(self):
+        g = self.g
+        for dz in range(1, g.Z):
+            self.arrive(self.z_in.at[dz], 4 + g.Z * (g.Y - 1) + dz - 1)
+        total = self.z_sum[g.z].astype(jnp.float32)
+        for dz in range(1, g.Z):
+            total += self.z_in[dz].astype(jnp.float32)
+        self.f_out[...] = total.astype(jnp.bfloat16)
+        if g.H > 1:
+            self.over_far()
+        self.push(self.f_out, self.f_in, 2, g.x_peer())
+
+    def over_far(self):
+        g = self.g
+        base = 4 + g.Z * (g.Y - 1) + g.Z - 2
+        self.far[g.h] = self.f_out[...]
+        for dh in range(1, g.H):
+            self.push(self.f_out, self.far.at[g.h], base + dh, g.far_peer(dh))
+        for dh in range(1, g.H):
+            self.arrive(self.far.at[g.far_index(-dh)], base + dh)
+        for copy in self.sent[1 - g.H :]:
+            copy.wait_send()
+        del self.sent[1 - g.H :]
+        total = self.far[0].astype(jnp.float32)
+        for h in range(1, g.H):
+            total += self.far[h].astype(jnp.float32)
+        self.f_out[...] = total.astype(jnp.bfloat16)
+
+    def over_core(self):
+        g = self.g
+        self.arrive(self.f_in, 2)
+        shared_out = lanes((1 - g.x) * self.apart, self.shared)
+        shared_in = lanes(g.x * self.apart, self.shared)
+        own = lanes(g.x * self.shared, self.apart)
+        other = lanes((1 - g.x) * self.shared, self.apart)
+        e = self.e_out.at[0]
+        e[:, lanes(self.apart, self.shared)] = plus(self.f_out[:, shared_out], self.f_in[:, shared_in])
+        e[:, self.x_keep] = self.f_out[:, own]
+        e[:, self.x_give] = self.f_in[:, other]
+        self.push(e, self.e_out.at[1], 3, g.core_peer())
+
+    def finish(self):
+        self.arrive(self.e_out.at[1], 3)
+        self.out[self.rows, self.out_keep] = self.e_out[0].astype(jnp.float32)
+        self.out[self.rows, self.out_give] = self.e_out[1].astype(jnp.float32)
+
+    def drain(self):
+        for copy in self.sent:
+            copy.wait_send()
+
+
+def plus(left, right):
+    return (left.astype(jnp.float32) + right.astype(jnp.float32)).astype(jnp.bfloat16)
+
+
+def scatter_kernel(grid, pieces, *refs):
+    n = len(pieces)
+    count = refs_count(pieces)
+    sources, outs = refs[:count], refs[count : 2 * count]
+    bufs = refs[2 * count : 2 * count + 10 * n]
+    send, recv, local = refs[2 * count + 10 * n :]
+    grid.locate()
+    grid.greet()
+    chunks = [
+        Scatter(
+            grid,
+            sources[which],
+            outs[which],
+            pl.ds(row, rows),
+            col,
+            width,
+            apart,
+            bufs[10 * i : 10 * i + 10],
+            send.at[i],
+            recv.at[i],
+            local.at[i],
+        )
+        for i, (which, row, rows, col, width, apart) in enumerate(pieces)
+    ]
+    for chunk in chunks:
+        chunk.begin()
+    stages = ["over_x", "over_y", "over_z", "over_pair", "over_core", "finish"]
+    for step in range(n + len(stages) - 1):
+        for depth, stage in enumerate(stages):
+            if 0 <= step - depth < n:
+                getattr(chunks[step - depth], stage)()
+    for chunk in chunks:
+        chunk.drain()
+
+
+def scatter_all(fsdp, dp, arrays):
+    grid = Grid(fsdp, dp)
+    pieces = []
+    for which, array in enumerate(arrays):
+        rows, width = array.shape[1:]
+        if width == 3072:
+            pieces += [(which, 0, rows, col, 1536, 128) for col in (0, 1536)]
+        elif width == 2304:
+            pieces += [(which, 0, rows, 0, 1536, 128), (which, 0, rows, 1536, 768, 128)]
+        elif rows * fsdp > 768:
+            pieces += [(which, row, rows // 2, 0, width, 128) for row in (0, rows // 2)]
+        else:
+            pieces.append((which, 0, rows, 0, width, 128))
+    count = Scatter.count(grid)
+    hbm = pl.BlockSpec(memory_space=pltpu.HBM)
+    vmem = pl.BlockSpec(memory_space=pltpu.VMEM)
+    scratch = []
+    for _, _, rows, _, width, apart in pieces:
+        scratch += Scatter.buffers(grid, rows, width, apart)
+    return pl.pallas_call(
+        functools.partial(scatter_kernel, grid, pieces),
+        out_shape=[jax.ShapeDtypeStruct(a.shape[1:], jnp.float32) for a in arrays],
+        in_specs=[hbm] * len(arrays),
+        out_specs=[vmem] * len(arrays),
+        scratch_shapes=scratch
+        + [
+            pltpu.SemaphoreType.DMA((len(pieces), count)),
+            pltpu.SemaphoreType.DMA((len(pieces), count)),
+            pltpu.SemaphoreType.DMA((len(pieces),)),
+        ],
+        compiler_params=pltpu.CompilerParams(
+            collective_id=1, has_side_effects=True, vmem_limit_bytes=56 * 1024 * 1024
+        ),
+        name="scatter_gradients",
+    )(*arrays)
 
 
 NORM_EPSILON = 1e-06
@@ -50,34 +527,28 @@
     reduce_weight,
     reduce_bias,
 ):
-    gathered = (
-        lax.all_gather(first_gain, "fsdp", axis=0, tiled=True),
-        lax.all_gather(first_shift, "fsdp", axis=0, tiled=True),
-        lax.all_gather(triple_weight, "fsdp", axis=0, tiled=True),
-        lax.all_gather(head_bias, "fsdp", axis=0, tiled=True),
-        lax.all_gather(output_weight, "fsdp", axis=0, tiled=True),
-        lax.all_gather(output_bias, "fsdp", axis=0, tiled=True),
-        lax.all_gather(second_gain, "fsdp", axis=0, tiled=True),
-        lax.all_gather(second_shift, "fsdp", axis=0, tiled=True),
-        lax.all_gather(expand_weight, "fsdp", axis=0, tiled=True),
-        lax.all_gather(expand_bias, "fsdp", axis=0, tiled=True),
-        lax.all_gather(reduce_weight, "fsdp", axis=0, tiled=True),
-        lax.all_gather(reduce_bias, "fsdp", axis=0, tiled=True),
-    )
-    (
-        gain_one,
-        shift_one,
-        triple,
-        biases,
-        project,
-        project_bias,
-        gain_two,
-        shift_two,
-        expand,
-        expand_add,
-        shrink,
-        shrink_add,
-    ) = gathered
+    fsdp, dp = lax.axis_size("fsdp"), lax.axis_size("dp")
+    small = (
+        first_gain,
+        first_shift,
+        head_bias,
+        output_bias,
+        second_gain,
+        second_shift,
+        expand_bias,
+        reduce_bias,
+    )
+    packed = jnp.stack([jnp.pad(item, (0, 768 - item.shape[0])) for item in small])
+    packed, triple, project, expand, shrink = gather_all(
+        fsdp, dp, (packed, triple_weight, output_weight, expand_weight, reduce_weight)
+    )
+    gain_one, shift_one, biases, project_bias, gain_two, shift_two, expand_add, shrink_add = (
+        packed[:, index, : item.shape[0]].reshape(-1) for index, item in enumerate(small)
+    )
+    triple = triple.reshape(-1, triple.shape[-1])
+    project = project.reshape(-1, project.shape[-1])
+    expand = expand.reshape(-1, expand.shape[-1])
+    shrink = shrink.reshape(-1, shrink.shape[-1])
     pairs, length, width = inputs.shape
     positions = lax.broadcasted_iota(jnp.int32, (pairs, length), 1)
     valid_rows = (positions < TEXT + patch_count[:, None]).astype(jnp.float32)
@@ -124,14 +595,8 @@
     activated = jax.nn.gelu(pre_act, approximate=False).astype(jnp.bfloat16)
     mixed = project_rows(activated, shrink) + shrink_add.astype(jnp.float32)
     layer_output = (valid_rows[..., None] * (middle + mixed)).astype(jnp.bfloat16)
-    gain_one_back, triple_back, project_back, gain_two_back, expand_back, shrink_back = (
-        lax.all_gather(first_gain, "fsdp", axis=0, tiled=True),
-        lax.all_gather(triple_weight, "fsdp", axis=0, tiled=True),
-        lax.all_gather(output_weight, "fsdp", axis=0, tiled=True),
-        lax.all_gather(second_gain, "fsdp", axis=0, tiled=True),
-        lax.all_gather(expand_weight, "fsdp", axis=0, tiled=True),
-        lax.all_gather(reduce_weight, "fsdp", axis=0, tiled=True),
-    )
+    gain_one_back, triple_back, project_back = gain_one, triple, project
+    gain_two_back, expand_back, shrink_back = gain_two, expand, shrink
     upstream = cotangent.astype(jnp.float32) * valid_rows[..., None]
     upstream_low = upstream.astype(jnp.bfloat16)
     shrink_add_grad = row_total(upstream_low)
@@ -194,61 +659,61 @@
     )
     input_part, gain_one_grad, shift_one_grad = norm_back_one(hidden_one_grad)
     input_gradient = (middle_grad + input_part).astype(jnp.bfloat16)
-    shares = (
-        lax.psum_scatter(
-            gain_one_grad.astype(jnp.bfloat16), "fsdp", scatter_dimension=0, tiled=True
-        ).astype(jnp.float32),
-        lax.psum_scatter(
-            shift_one_grad.astype(jnp.bfloat16), "fsdp", scatter_dimension=0, tiled=True
-        ).astype(jnp.float32),
-        lax.psum_scatter(
-            triple_grad.astype(jnp.bfloat16), "fsdp", scatter_dimension=0, tiled=True
-        ).astype(jnp.float32),
-        lax.psum_scatter(
-            head_bias_grad.astype(jnp.bfloat16), "fsdp", scatter_dimension=0, tiled=True
-        ).astype(jnp.float32),
-        lax.psum_scatter(
-            project_grad.astype(jnp.bfloat16), "fsdp", scatter_dimension=0, tiled=True
-        ).astype(jnp.float32),
-        lax.psum_scatter(
-            project_bias_grad.astype(jnp.bfloat16), "fsdp", scatter_dimension=0, tiled=True
-        ).astype(jnp.float32),
-        lax.psum_scatter(
-            gain_two_grad.astype(jnp.bfloat16), "fsdp", scatter_dimension=0, tiled=True
-        ).astype(jnp.float32),
-        lax.psum_scatter(
-            shift_two_grad.astype(jnp.bfloat16), "fsdp", scatter_dimension=0, tiled=True
-        ).astype(jnp.float32),
-        lax.psum_scatter(
-            expand_grad.astype(jnp.bfloat16), "fsdp", scatter_dimension=0, tiled=True
-        ).astype(jnp.float32),
-        lax.psum_scatter(
-            expand_add_grad.astype(jnp.bfloat16), "fsdp", scatter_dimension=0, tiled=True
-        ).astype(jnp.float32),
-        lax.psum_scatter(
-            shrink_grad.astype(jnp.bfloat16), "fsdp", scatter_dimension=0, tiled=True
-        ).astype(jnp.float32),
-        lax.psum_scatter(
-            shrink_add_grad.astype(jnp.bfloat16), "fsdp", scatter_dimension=0, tiled=True
-        ).astype(jnp.float32),
-    )
-    totals = tuple(
-        (
-            lax.psum(shares[0].astype(jnp.bfloat16), "dp").astype(jnp.float32),
-            lax.psum(shares[1].astype(jnp.bfloat16), "dp").astype(jnp.float32),
-            lax.psum(shares[2].astype(jnp.bfloat16), "dp").astype(jnp.float32),
-            lax.psum(shares[3].astype(jnp.bfloat16), "dp").astype(jnp.float32),
-            lax.psum(shares[4].astype(jnp.bfloat16), "dp").astype(jnp.float32),
-            lax.psum(shares[5].astype(jnp.bfloat16), "dp").astype(jnp.float32),
-            lax.psum(shares[6].astype(jnp.bfloat16), "dp").astype(jnp.float32),
-            lax.psum(shares[7].astype(jnp.bfloat16), "dp").astype(jnp.float32),
-            lax.psum(shares[8].astype(jnp.bfloat16), "dp").astype(jnp.float32),
-            lax.psum(shares[9].astype(jnp.bfloat16), "dp").astype(jnp.float32),
-            lax.psum(shares[10].astype(jnp.bfloat16), "dp").astype(jnp.float32),
-            lax.psum(shares[11].astype(jnp.bfloat16), "dp").astype(jnp.float32),
+    small_grads = (
+        gain_one_grad,
+        shift_one_grad,
+        head_bias_grad,
+        project_bias_grad,
+        gain_two_grad,
+        shift_two_grad,
+        expand_add_grad,
+        shrink_add_grad,
+    )
+    packed_grad = jnp.stack(
+        [
+            jnp.pad(
+                item.astype(jnp.bfloat16).reshape(fsdp, -1),
+                ((0, 0), (0, 768 - item.shape[0] // fsdp)),
+            )
+            for item in small_grads
+        ],
+        axis=1,
+    )
+    shares = scatter_all(
+        fsdp,
+        dp,
+        tuple(
+            item.astype(jnp.bfloat16).reshape(fsdp, -1, item.shape[-1])
+            for item in (shrink_grad, expand_grad, project_grad, triple_grad)
         )
-    )
-    return (layer_output, input_gradient) + tuple(totals)
+        + (packed_grad,),
+    )
+    (
+        gain_one_sum,
+        shift_one_sum,
+        head_bias_sum,
+        project_bias_sum,
+        gain_two_sum,
+        shift_two_sum,
+        expand_add_sum,
+        shrink_add_sum,
+    ) = (shares[4][index, : item.shape[0] // fsdp] for index, item in enumerate(small_grads))
+    return (
+        layer_output,
+        input_gradient,
+        gain_one_sum,
+        shift_one_sum,
+        shares[3],
+        head_bias_sum,
+        shares[2],
+        project_bias_sum,
+        gain_two_sum,
+        shift_two_sum,
+        shares[1],
+        expand_add_sum,
+        shares[0],
+        shrink_add_sum,
+    )
 
 
 def solution(mesh):

time: 768 us -> 518 us (0.67)
  waiting for transfers between devices: 329 us -> 0 us
  Pallas kernels: 0 us -> 177 us
  blocking collectives: 97.3 us -> 0 us
  between operations: 18 us -> 1.53 us
  local copies, waits for them, and re-layouts: 50.5 us -> 64 us
    reduce_scatter x4 -> x0, waiting for transfers between devices: 191 us -> none  [the longest x1 98.7 us: shards(): lax.psum_scatter(shrink_grad.astype(jnp.bfloat16), 'fsdp', scatter_dimens...]
    pallas_call x0 -> x2, Pallas kernels: none -> 177 us  [the longest x1 99.1 us: scatter_all(): pl.pallas_call(functools.partial(scatter_kernel, grid, pieces), out_shape...]
    all_gather x4 -> x0, waiting for transfers between devices: 90.9 us -> none  [the longest x1 62.9 us: shards(): lax.all_gather(expand_weight, 'fsdp', axis=0, tiled=True)]
    unnamed x2 -> x0, blocking collectives: 61.3 us -> none
    psum x1 -> x0, waiting for transfers between devices: 44.1 us -> none  [shards(): lax.psum(shares[2].astype(jnp.bfloat16), 'dp').astype(jnp.float32)]
    all_gather x1 -> x0, blocking collectives: 23.1 us -> none  [shards(): lax.all_gather(expand_bias, 'fsdp', axis=0, tiled=True)]
    psum x1 -> x0, blocking collectives: 12.9 us -> none  [shards(): lax.psum(shares[0].astype(jnp.bfloat16), 'dp').astype(jnp.float32)]
    convert_element_type x17 -> x1, other arithmetic: 13.4 us -> 0.77 us  [shards(): biases_wide = biases.astype(jnp.float32)]
  transfers between devices with their start and end apart: 9 -> 0, of which waited for: 5 -> 0; matrix products, arithmetic and copies ran while one was open for 29% -> 0% of each run, Pallas kernels for 0% -> 0%
where the time goes in v1:
time: 518 us; the launch traced here: 513 us
  matrix products  178 us (34%)
  Pallas kernels  177 us (34%)
  other arithmetic  92.8 us (18%)
  local copies, waits for them, and re-layouts  64 us (12%)
    pallas_call x1, Pallas kernels, scatter_all(): pl.pallas_call(functools.partial(scatter_kernel, grid, pieces), out_shape...  99.1 us
    pallas_call x1, Pallas kernels, gather_all(): pl.pallas_call(functools.partial(gather_kernel, grid, pieces), out_shape=...  78.1 us
    dot_general x4, matrix products, back_rows(): jnp.einsum('pse,de->psd', left, right, preferred_element_type=jnp.float32)  43.3 us
    dot_general x4, matrix products, project_rows(): jnp.einsum('psd,de->pse', left, right, preferred_element_type=jnp.float32)  35.8 us
    convert_element_type x1, other arithmetic, shards(): activated = jax.nn.gelu(pre_act, approximate=False).astype(jnp.bfloat16)  32.8 us
    dot_general x4, matrix products, outer_rows(): jnp.einsum('psd,pse->de', left, right, preferred_element_type=jnp.float32)  31.5 us
    convert_element_type x1, other arithmetic, shards(): score_grad = (probs_again * (probs_grad - jnp.sum(probs_again * probs_gra...  19.6 us
    dot_general x1, matrix products, shards(): jnp.einsum('pshd,pthd->phst', context_grad, value_rows, preferred_element...  16.8 us

profile of v1, /device:TPU:1, one launch (start us, length us, event | category | flops | bytes accessed | tf_op | source)
XLA Modules:
  0.0 513.2 jit_solution(8671592626231439531)
XLA Ops:
  0.7 0.8 broadcast_add_fusion
  5.4 0.7 pad.60
  7.5 1.8 convert_reduce_fusion
  9.3 2.1 fusion.22
  12.6 78.1 %gather_weights.1 = (bf16[8,8,768]{2,1,0:T(8,128)(2,1)}, bf16[8,96,2304]{2,1,0:T(8,128)(2,1)}, bf16[8,96,768]{2,1,0:T(8,128)(2,1)}, bf16[8,96,3072]{2,1,0:T(8,128)(2,1)}, bf16[8,384,768]{2,1,0:T(8,128)(2,1)}) custom-call(bf16[8,768]{1,0:T(8,128)(2,1)} %stack.62.refs_0_, bf16[96,2304]{1,0:T(8,128)(2,1)} %refs_1_.1, bf16[96,768]{1,0:T(8,128)(2,1)} %refs_2_.1, ...), custom_call_target="tpu_custom_call" | custom-call | tf_op jit(solution)/shard_map/gather_weights/pallas_call | solution.py:240
  90.7 0.8 slice_convert_fusion.1
  91.7 0.8 slice_convert_fusion
  92.5 1.1 convert_reduce_fusion.1
  93.6 0.7 reshape.304
  94.5 0.7 reshape.302
  95.3 7.3 %add_convert_fusion.1 = bf16[4,280,2304]{2,1,0:T(8,128)(2,1)S(1)} fusion(bf16[768,2304,1]{1,0,2:T(8,128)(2,1)} %bitcast.119, f32[2304]{0:T(1024)S(1)} %pad_maximum_fusion.1, bf16[4,280,768]{2,1,0:T(8,128)(2,1)S(1)} %copy-done.3, f32[768]{0:T(1024)S(1)} %reshape.299, f32[768]{0:T(1024)S(1)} %reshape.298, f32[4,280]{1,0:T(4,128)S(1)} %fusion.45, ...), kind=kOutput, calls=%fused_computation.31 | convolution fusion | flops 3973939200 | bytes 10444544 | tf_op jit(solution)/shard_map/psd,de->pse/dot_general | solution.py:498
  102.7 2.1 fusion.58
  104.8 2.4 copy.48
  107.2 2.8 copy.47
  110.1 4.4 copy.46
  114.4 11.1 %fusion.12 = (f32[4,12,280]{2,1,0:T(8,128)S(1)}, f32[4,12,280,280]{2,3,1,0:T(8,128)}) fusion(pred[4,280]{1,0:T(4,128)(4,1)S(1)} %get-tuple-element.70, bf16[4,280,12,64]{1,3,2,0:T(8,128)(2,1)S(1)} %bitcast.96, bf16[4,280,12,64]{1,3,2,0:T(8,128)(2,1)} %bitcast.98), kind=kOutput, calls=%fused_computation.35 | convolution fusion | flops 492965760 | bytes 18548320 | tf_op jit(solution)/shard_map/pshd,pthd->phst/dot_general | solution.py:572
  125.5 11.0 %fusion = f32[4,12,280]{2,1,0:T(8,128)S(1)} fusion(f32[4,12,280]{2,1,0:T(8,128)S(1)} %get-tuple-element.71, f32[4,12,280,280]{2,3,1,0:T(8,128)} %get-tuple-element.72, pred[4,280]{1,0:T(4,128)(4,1)S(1)} %get-tuple-element.70), kind=kLoop, calls=%fused_computation.7 | loop fusion | flops 15039360 | bytes 15161440 | tf_op jit(solution)/shard_map/reduce_sum | solution.py:580
  137.1 1.2 copy-done
  138.4 8.6 %fusion.28 = bf16[4,12,64,280]{3,2,1,0:T(8,128)(2,1)} fusion(bf16[4,280,12,64]{1,3,2,0:T(8,128)(2,1)} %bitcast.101, f32[4,12,280]{2,1,0:T(8,128)} %copy-done.17, f32[4,12,280]{2,1,0:T(8,128)S(1)} %get-tuple-element.71, f32[4,12,280,280]{2,3,1,0:T(8,128)S(1)} %copy-done, pred[4,280]{1,0:T(4,128)(4,1)S(1)} %get-tuple-element.70), kind=kOutput, calls=%fused_computation.69 | convolution fusion | flops 501365760 | bytes 18602080 | tf_op jit(solution)/shard_map/phst,pthd->pshd/dot_general | solution.py:583
  147.0 4.0 fusion.60
  151.5 1.2 copy-done.8
  153.3 14.3 %fusion.27 = (u8[280,3072]{1,0:T(8,128)(4,1)S(1)}, u8[280,3072]{1,0:T(8,128)(4,1)S(1)}, f32[4,280,3072]{2,1,0:T(8,128)S(1)}) fusion(f32[3072]{0:T(1024)S(1)} %bitcast.111, bf16[768,3072,1]{1,0,2:T(8,128)(2,1)} %bitcast.115, f32[4,280,768]{2,1,0:T(8,128)} %copy-done.8, f32[768]{0:T(1024)S(1)} %copy-done.43, f32[768]{0:T(1024)S(1)} %reshape.301, ...), kind=kOutput, calls=%fused_computation.67 | convolution fusion | flops 5335572480 | bytes 23669504 | tf_op jit(solution)/shard_map/psd,de->pse/dot_general | solution.py:498
  167.7 32.8 %multiply_convert_fusion.1 = (bf16[4,280,3072]{2,1,0:T(8,128)(2,1)}, f32[4,280,3072]{2,1,0:T(8,128)}) fusion(f32[4,280,3072]{2,1,0:T(8,128)S(1)} %get-tuple-element.75, f32[3072]{0:T(1024)S(1)} %bitcast.112, u8[280,3072]{1,0:T(8,128)(4,1)S(1)} %get-tuple-element.35, u8[280,3072]{1,0:T(8,128)(4,1)S(1)} %get-tuple-element.34), kind=kLoop, calls=%fused_computation.16 | loop fusion | flops 244285440 | bytes 36139008 | tf_op jit(solution)/shard_map/convert_element_type | solution.py:595
  200.5 19.0 %fusion.61 = (bf16[3072]{0:T(1024)(128)(2,1)}, bf16[4,280,3072]{2,1,0:T(8,128)(2,1)}) fusion(f32[4,280,3072]{2,1,0:T(8,128)} %get-tuple-element.56, bf16[3072,768,1]{1,0,2:T(8,128)(2,1)} %bitcast.117, bf16[4,280,768]{2,1,0:T(8,128)(2,1)} %param.17, f32[4,280]{1,0:T(4,128)} %get-tuple-element.69, f32[4,280,3072]{2,1,0:T(8,128)} %copy-done.7, f32[3072]{0:T(1024)} %bitcast.113), kind=kOutput, calls=%fused_computation.133 | convolution fusion | flops 5342450688 | bytes 40868224 | tf_op jit(solution)/shard_map/pse,de->psd/dot_general | solution.py:502
  219.5 10.2 %multiply_convert_fusion.4 = bf16[4,280,768]{2,1,0:T(8,128)(2,1)} fusion(f32[4,280,768]{2,1,0:T(8,128)S(1)} %copy-done.9, bf16[4,280,3072]{2,1,0:T(8,128)(2,1)} %get-tuple-element.55, bf16[3072,768,1]{1,0,2:T(8,128)(2,1)} %bitcast.118, f32[768]{0:T(1024)} %reshape.304, f32[4,280]{1,0:T(4,128)} %get-tuple-element.69), kind=kOutput, calls=%fused_computation.63 | convolution fusion | flops 5288263680 | bytes 16768384 | tf_op jit(solution)/shard_map/psd,de->pse/dot_general | solution.py:498
  229.7 9.1 %bitcast_convert_fusion.1 = bf16[3072,768]{1,0:T(8,128)(2,1)} fusion(bf16[4,280,3072]{2,1,0:T(8,128)(2,1)S(1)} %copy-done.11, bf16[4,280,768]{2,1,0:T(8,128)(2,1)S(1)} %copy-done.12, f32[4,280]{1,0:T(4,128)S(1)} %copy-done.30), kind=kOutput, calls=%fused_computation.34 | convolution fusion | flops 5289762816 | bytes 13324672 | tf_op jit(solution)/shard_map/psd,pse->de/dot_general | solution.py:506
  238.8 10.9 %multiply_reduce_fusion.1 = (bf16[768]{0:T(1024)(128)(2,1)}, f32[4,280]{1,0:T(4,128)}, bf16[768]{0:T(1024)(128)(2,1)}, f32[4,280,768]{2,1,0:T(8,128)}) fusion(f32[4,280,768]{2,1,0:T(8,128)S(1)} %copy-done.9, f32[4,280]{1,0:T(4,128)S(1)} %copy-done.37, f32[4,280]{1,0:T(4,128)S(1)} %broadcast_multiply_fusion, f32[768]{0:T(1024)S(1)} %reshape.301, ...), kind=kOutput, calls=%fused_computation.57 | convolution fusion | flops 5291701248 | bytes 18500736 | tf_op jit(solution)/shard_map/pse,de->psd/dot_general | solution.py:502
  249.7 1.3 reshape.296
  251.0 1.3 convert_element_type.261
  252.3 0.7 multiply_multiply_fusion.6
  253.1 3.8 fusion.56
  257.1 11.4 %bitcast_convert_fusion = bf16[768,3072]{1,0:T(8,128)(2,1)} fusion(bf16[4,280,3072]{2,1,0:T(8,128)(2,1)} %get-tuple-element.81, f32[4,280,768]{2,1,0:T(8,128)S(1)} %copy-done.10, f32[768]{0:T(1024)S(1)} %copy-done.44, f32[768]{0:T(1024)S(1)} %reshape.301, f32[4,280]{1,0:T(4,128)S(1)} %copy-done.38, f32[4,280]{1,0:T(4,128)S(1)} %broadcast_multiply_fusion), kind=kOutput, calls=%fused_computation.33 | convolution fusion | flops 5291483136 | bytes 15055616 | tf_op jit(solution)/shard_map/psd,pse->de/dot_general | solution.py:506
  268.5 0.8 convert_element_type.263
  269.2 0.8 pad_bitcast_fusion.1
  270.1 0.7 pad_bitcast_fusion.3
  272.6 2.9 fusion.54
  275.5 2.7 bitcast_convert_fusion.3
  278.2 0.8 reshape.295
  280.4 4.5 convolution_convert_fusion
  284.9 4.1 copy.51
  289.1 14.0 %fusion.29 = bf16[4,12,64,280]{3,2,1,0:T(8,128)(2,1)} fusion(bf16[4,280,12,64]{1,3,2,0:T(8,128)(2,1)} %bitcast.103, f32[4,12,280]{2,1,0:T(8,128)S(1)} %log_add_fusion, f32[4,12,280,280]{2,3,1,0:T(8,128)} %get-tuple-element.72, pred[4,280]{1,0:T(4,128)(4,1)S(1)} %get-tuple-element.70), kind=kOutput, calls=%fused_computation.70 | convolution fusion | flops 497602560 | bytes 18548320 | tf_op jit(solution)/shard_map/phst,pshd->pthd/dot_general | solution.py:625
  303.0 4.0 copy.57
  307.1 16.8 %multiply_reduce_fusion = (f32[4,12,280]{2,1,0:T(8,128)S(1)}, f32[4,12,280,280]{2,3,1,0:T(8,128)}) fusion(f32[4,12,280]{2,1,0:T(8,128)S(1)} %log_add_fusion, f32[4,12,280,280]{2,3,1,0:T(8,128)} %get-tuple-element.72, pred[4,280]{1,0:T(4,128)(4,1)S(1)} %get-tuple-element.70, bf16[4,280,12,64]{1,3,2,0:T(8,128)(2,1)} %bitcast.104, ...), kind=kOutput, calls=%fused_computation.1 | convolution fusion | flops 500492160 | bytes 33654880 | tf_op jit(solution)/shard_map/pshd,pthd->phst/dot_general | solution.py:631
  323.9 19.6 %multiply_convert_fusion = bf16[4,12,280,280]{2,3,1,0:T(8,128)(2,1)} fusion(f32[4,12,280,280]{2,3,1,0:T(8,128)} %get-tuple-element.78, f32[4,12,280]{2,1,0:T(8,128)S(1)} %get-tuple-element.77, f32[4,12,280]{2,1,0:T(8,128)S(1)} %log_add_fusion, f32[4,12,280,280]{2,3,1,0:T(8,128)} %get-tuple-element.72, pred[4,280]{1,0:T(4,128)(4,1)S(1)} %get-tuple-element.70), kind=kLoop, calls=%fused_computation | loop fusion | flops 22579200 | bytes 37740640 | tf_op jit(solution)/shard_map/convert_element_type | solution.py:636
  343.5 9.0 %multiply_convert_fusion.2 = bf16[4,12,64,280]{3,2,1,0:T(8,128)(2,1)} fusion(bf16[4,280,12,64]{1,3,2,0:T(8,128)(2,1)S(1)} %bitcast.97, bf16[4,12,280,280]{2,3,1,0:T(8,128)(2,1)} %multiply_convert_fusion), kind=kOutput, calls=%fused_computation.47 | convolution fusion | flops 483409920 | bytes 10967040 | tf_op jit(solution)/shard_map/phst,pshd->pthd/dot_general | solution.py:642
  352.5 7.7 %multiply_convert_fusion.3 = bf16[4,12,64,280]{3,2,1,0:T(8,128)(2,1)} fusion(bf16[4,280,12,64]{1,3,2,0:T(8,128)(2,1)S(1)} %bitcast.99, bf16[4,12,280,280]{2,3,1,0:T(8,128)(2,1)} %multiply_convert_fusion), kind=kOutput, calls=%fused_computation.48 | convolution fusion | flops 483409920 | bytes 10967040 | tf_op jit(solution)/shard_map/phst,pthd->pshd/dot_general | solution.py:638
  360.2 4.1 copy.55
  364.3 4.1 copy.56
  368.4 8.9 %fusion.53 = (bf16[768]{0:T(1024)(128)(2,1)S(1)}, f32[4,280]{1,0:T(4,128)S(1)}, f32[4,280,768]{2,1,0:T(8,128)}) fusion(f32[768]{0:T(1024)S(1)} %copy-done.35, f32[4,280]{1,0:T(4,128)S(1)} %copy-done.23, bf16[4,280,768]{2,1,0:T(8,128)(2,1)} %param.15, bf16[768,2304,1]{1,0,2:T(8,128)(2,1)} %bitcast.120, bf16[4,280,768]{2,1,0:T(8,128)(2,1)} %copy.57, ...), kind=kOutput, calls=%fused_computation.127 | convolution fusion | flops 3984259328 | bytes 13874432 | tf_op jit(solution)/shard_map/pse,de->psd/dot_general | solution.py:502
  377.4 0.7 convert_element_type.258
  378.0 4.6 fusion.51
  382.7 8.3 %bitcast_convert_fusion.2 = bf16[768,2304]{1,0:T(8,128)(2,1)} fusion(bf16[4,280,768]{2,1,0:T(8,128)(2,1)S(1)} %copy-done.5, f32[768]{0:T(1024)S(1)} %copy-done.42, f32[768]{0:T(1024)S(1)} %copy-done.35, f32[4,280]{1,0:T(4,128)S(1)} %copy-done.28, f32[4,280]{1,0:T(4,128)S(1)} %copy-done.23, bf16[4,280,768]{2,1,0:T(8,128)(2,1)S(1)} %copy-done.13, ...), kind=kOutput, calls=%fused_computation.36 | convolution fusion | flops 3986030592 | bytes 10435328 | tf_op jit(solution)/shard_map/psd,pse->de/dot_general | solution.py:506
  391.8 3.3 fusion.21
  395.1 0.7 convert_element_type.256
  395.9 4.9 add_convert_fusion.2
  400.9 1.7 stack.71.refs_4_
  402.6 99.1 %scatter_gradients.1 = (f32[384,768]{1,0:T(8,128)}, f32[96,3072]{1,0:T(8,128)}, f32[96,768]{1,0:T(8,128)}, f32[96,2304]{1,0:T(8,128)}, f32[8,768]{1,0:T(8,128)}) custom-call(bf16[8,384,768]{2,1,0:T(8,128)(2,1)} %bitcast.106, bf16[8,96,3072]{2,1,0:T(8,128)(2,1)} %bitcast.107, bf16[8,96,768]{2,1,0:T(8,128)(2,1)} %bitcast.110, bf16[8,96,2304]{2,1,0:T(8,128)(2,1)} %bitcast.108, ...), custom_call_target="tpu_custom_call" | custom-call | tf_op jit(solution)/shard_map/scatter_gradients/pallas_call | solution.py:470
  501.7 1.4 slice.110
  503.0 1.3 slice_reduce_fusion.2
  504.3 1.4 slice_bitcast_fusion
  505.8 2.1 copy.77
  507.9 1.7 copy.78
  509.6 2.4 copy.79
  512.0 1.0 copy.80
  (145 shorter events, 13.3 us)
Async XLA Ops:
  0.6 94.6 %copy-start.3 = (bf16[4,280,768]{2,1,0:T(8,128)(2,1)S(1)}, bf16[4,280,768]{2,1,0:T(8,128)(2,1)}, u32[]{:S(2)}) copy-start(bf16[4,280,768]{2,1,0:T(8,128)(2,1)} %param.15) | copy-start | bytes 5160964
  9.2 93.4 %copy-start.22 = (f32[4,280]{1,0:T(4,128)}, f32[4,280]{1,0:T(4,128)S(1)}, u32[]{:S(2)}) copy-start(f32[4,280]{1,0:T(4,128)S(1)} %broadcast_multiply_fusion.1) | copy-start | bytes 13444
  11.3 0.6 copy-start.24
  12.0 90.7 %copy-start.27 = (f32[4,280]{1,0:T(4,128)}, f32[4,280]{1,0:T(4,128)S(1)}, u32[]{:S(2)}) copy-start(f32[4,280]{1,0:T(4,128)S(1)} %fusion.45) | copy-start | bytes 13444
  92.5 75.2 %copy-start.32 = (f32[8,1,384]{2,1,0:T(1,128)}, f32[8,1,384]{2,1,0:T(1,128)S(1)}, u32[]{:S(2)}) copy-start(f32[8,1,384]{2,1,0:T(1,128)S(1)} %slice_convert_fusion) | copy-start | bytes 36868
  94.4 8.3 %copy-start.34 = (f32[768]{0:T(1024)}, f32[768]{0:T(1024)S(1)}, u32[]{:S(2)}) copy-start(f32[768]{0:T(1024)S(1)} %reshape.298) | copy-start | bytes 9220
  95.2 7.5 %copy-start.41 = (f32[768]{0:T(1024)}, f32[768]{0:T(1024)S(1)}, u32[]{:S(2)}) copy-start(f32[768]{0:T(1024)S(1)} %reshape.299) | copy-start | bytes 9220
  110.0 15.4 %copy-start.1 = (bf16[4,280,768]{1,2,0:T(8,128)(2,1)}, bf16[4,280,768]{1,2,0:T(8,128)(2,1)S(1)}, u32[]{:S(2)}) copy-start(bf16[4,280,768]{1,2,0:T(8,128)(2,1)S(1)} %copy.47) | copy-start | bytes 5160964
  125.5 12.9 %copy-start = (f32[4,12,280,280]{2,3,1,0:T(8,128)S(1)}, f32[4,12,280,280]{2,3,1,0:T(8,128)}, u32[]{:S(2)}) copy-start(f32[4,12,280,280]{2,3,1,0:T(8,128)} %get-tuple-element.72) | copy-start | bytes 45158404
  136.5 0.6 copy-start.17
  138.4 8.6 %copy-start.4 = (bf16[4,280,768]{2,1,0:T(8,128)(2,1)S(1)}, bf16[4,280,768]{2,1,0:T(8,128)(2,1)}, u32[]{:S(2)}) copy-start(bf16[4,280,768]{2,1,0:T(8,128)(2,1)} %param.15) | copy-start | bytes 5160964
  147.0 6.3 %copy-start.43 = (f32[768]{0:T(1024)S(1)}, f32[768]{0:T(1024)}, u32[]{:S(2)}) copy-start(f32[768]{0:T(1024)} %reshape.302) | copy-start | bytes 9220
  150.9 1.8 copy-start.8
  152.7 0.6 copy-start.26
  153.3 14.4 %copy-start.36 = (f32[4,280]{1,0:T(4,128)}, f32[4,280]{1,0:T(4,128)S(1)}, u32[]{:S(2)}) copy-start(f32[4,280]{1,0:T(4,128)S(1)} %fusion.46) | copy-start | bytes 13444
  167.7 32.8 %copy-start.7 = (f32[4,280,3072]{2,1,0:T(8,128)}, f32[4,280,3072]{2,1,0:T(8,128)S(1)}, u32[]{:S(2)}) copy-start(f32[4,280,3072]{2,1,0:T(8,128)S(1)} %get-tuple-element.75) | copy-start | bytes 41287684
  200.5 19.0 %copy-start.9 = (f32[4,280,768]{2,1,0:T(8,128)S(1)}, f32[4,280,768]{2,1,0:T(8,128)}, u32[]{:S(2)}) copy-start(f32[4,280,768]{2,1,0:T(8,128)} %copy-done.8) | copy-start | bytes 10321924
  219.5 10.2 %copy-start.11 = (bf16[4,280,3072]{2,1,0:T(8,128)(2,1)S(1)}, bf16[4,280,3072]{2,1,0:T(8,128)(2,1)}, u32[]{:S(2)}) copy-start(bf16[4,280,3072]{2,1,0:T(8,128)(2,1)} %get-tuple-element.55) | copy-start | bytes 20643844
  219.5 10.2 %copy-start.12 = (bf16[4,280,768]{2,1,0:T(8,128)(2,1)S(1)}, bf16[4,280,768]{2,1,0:T(8,128)(2,1)}, u32[]{:S(2)}) copy-start(bf16[4,280,768]{2,1,0:T(8,128)(2,1)} %param.17) | copy-start | bytes 5160964
  219.5 10.2 %copy-start.30 = (f32[4,280]{1,0:T(4,128)S(1)}, f32[4,280]{1,0:T(4,128)}, u32[]{:S(2)}) copy-start(f32[4,280]{1,0:T(4,128)} %get-tuple-element.69) | copy-start | bytes 13444
  229.7 9.1 %copy-start.37 = (f32[4,280]{1,0:T(4,128)S(1)}, f32[4,280]{1,0:T(4,128)}, u32[]{:S(2)}) copy-start(f32[4,280]{1,0:T(4,128)} %copy-done.36) | copy-start | bytes 13444
  229.7 9.1 %copy-start.46 = (bf16[4,280,3072]{2,1,0:T(8,128)(2,1)S(1)}, bf16[4,280,3072]{2,1,0:T(8,128)(2,1)}, u32[]{:S(2)}) copy-start(bf16[4,280,3072]{2,1,0:T(8,128)(2,1)} %get-tuple-element.81) | copy-start | bytes 20643844
  253.1 4.0 copy-start.10
  253.1 4.0 copy-start.38
  253.1 4.0 copy-start.44
  268.5 9.8 %copy-start.29 = (f32[4,280]{1,0:T(4,128)}, f32[4,280]{1,0:T(4,128)S(1)}, u32[]{:S(2)}) copy-start(f32[4,280]{1,0:T(4,128)S(1)} %negate_multiply_fusion.2) | copy-start | bytes 13444
  269.2 6.3 %copy-start.45 = (bf16[4,12,64,280]{3,2,1,0:T(8,128)(2,1)S(1)}, bf16[4,12,64,280]{3,2,1,0:T(8,128)(2,1)}, u32[]{:S(2)}) copy-start(bf16[4,12,64,280]{3,2,1,0:T(8,128)(2,1)} %fusion.28) | copy-start | bytes 5160964
  275.5 2.7 copy-start.15
  323.9 19.6 %copy-start.2 = (bf16[4,280,768]{1,2,0:T(8,128)(2,1)S(1)}, bf16[4,280,768]{1,2,0:T(8,128)(2,1)}, u32[]{:S(2)}) copy-start(bf16[4,280,768]{1,2,0:T(8,128)(2,1)} %copy-done.1) | copy-start | bytes 5160964
  343.5 9.0 %copy-start.6 = (bf16[4,280,768]{1,2,0:T(8,128)(2,1)S(1)}, bf16[4,280,768]{1,2,0:T(8,128)(2,1)}, u32[]{:S(2)}) copy-start(bf16[4,280,768]{1,2,0:T(8,128)(2,1)} %copy.48) | copy-start | bytes 5160964
  360.2 8.2 %copy-start.23 = (f32[4,280]{1,0:T(4,128)S(1)}, f32[4,280]{1,0:T(4,128)}, u32[]{:S(2)}) copy-start(f32[4,280]{1,0:T(4,128)} %copy-done.22) | copy-start | bytes 13444
  360.2 8.2 %copy-start.35 = (f32[768]{0:T(1024)S(1)}, f32[768]{0:T(1024)}, u32[]{:S(2)}) copy-start(f32[768]{0:T(1024)} %copy-done.34) | copy-start | bytes 9220
  368.4 8.9 %copy-start.25 = (f32[4,280]{1,0:T(4,128)S(1)}, f32[4,280]{1,0:T(4,128)}, u32[]{:S(2)}) copy-start(f32[4,280]{1,0:T(4,128)} %copy-done.24) | copy-start | bytes 13444
  377.3 5.3 %copy-start.28 = (f32[4,280]{1,0:T(4,128)S(1)}, f32[4,280]{1,0:T(4,128)}, u32[]{:S(2)}) copy-start(f32[4,280]{1,0:T(4,128)} %copy-done.27) | copy-start | bytes 13444
  377.3 5.3 %copy-start.42 = (f32[768]{0:T(1024)S(1)}, f32[768]{0:T(1024)}, u32[]{:S(2)}) copy-start(f32[768]{0:T(1024)} %copy-done.41) | copy-start | bytes 9220
  377.4 14.4 %copy-start.31 = (f32[4,280]{1,0:T(4,128)}, f32[4,280]{1,0:T(4,128)S(1)}, u32[]{:S(2)}) copy-start(f32[4,280]{1,0:T(4,128)S(1)} %multiply_multiply_fusion.5) | copy-start | bytes 13444
  378.0 4.6 copy-start.5
  378.0 4.6 copy-start.13
  378.0 4.7 copy-start.14
  395.8 4.9 copy-start.40
  395.8 4.9 copy-start.39
  395.8 5.0 copy-start.33
  395.8 5.1 copy-start.18
  395.8 5.1 copy-start.19
  395.8 5.1 copy-start.20
  395.8 5.1 copy-start.21
  501.7 10.3 %copy-start.16 = (f32[384,768]{1,0:T(8,128)S(1)}, f32[384,768]{1,0:T(8,128)}, u32[]{:S(2)}) copy-start(f32[384,768]{1,0:T(8,128)} %get-tuple-element.108) | copy-start | bytes 3538948

commit v2 on v1

--- a/solution.py
+++ b/solution.py
@@ -85,18 +85,18 @@
 
 
 class Gather:
-    def __init__(self, grid, src, dst, rows, col, width, send, recv):
-        self.g, self.src, self.dst, self.rows = grid, src, dst, rows
+    def __init__(self, grid, src, dst, depth, row, rows, col, width, send, recv):
+        self.g, self.src, self.dst = grid, src, dst
+        self.depth, self.row, self.rows = depth, row, rows
         self.send, self.recv = send, recv
-        self.half, self.group = width // 2, width // 6
-        self.col = col
+        half, group = width // 2, width // 6
         self.sent = []
         g = grid
-        self.mine = lanes(col + g.c * self.half + g.x * self.group, 2 * self.group)
-        self.x_out = lanes(col + g.c * self.half + 2 * g.x * self.group, self.group)
-        self.x_in = lanes(col + g.c * self.half + 2 * (1 - g.x) * self.group, self.group)
-        self.core_out = lanes(col + g.c * self.half, self.half)
-        self.core_in = lanes(col + (1 - g.c) * self.half, self.half)
+        self.mine = lanes(col + g.c * half + g.x * group, 2 * group)
+        self.x_out = lanes(col + g.c * half + 2 * g.x * group, group)
+        self.x_in = lanes(col + g.c * half + 2 * (1 - g.x) * group, group)
+        self.core_out = lanes(col + g.c * half, half)
+        self.core_in = lanes(col + (1 - g.c) * half, half)
         self.z_base, self.y_base = 0, g.Z - 1
         self.x_base = self.y_base + g.Z * (g.Y - 1)
         self.c_base = self.x_base + g.F - 1
@@ -106,7 +106,8 @@
         return grid.Z - 1 + grid.Z * (grid.Y - 1) + 2 * (grid.F - 1)
 
     def view(self, shard, columns):
-        return self.dst.at[shard, self.rows, columns]
+        start = pl.multiple_of(shard * self.depth + self.row, 8)
+        return self.dst.at[pl.ds(start, self.rows), columns]
 
     def push(self, src, dst, index, peer):
         copy = remote(src, dst, self.send.at[index], self.recv.at[index], peer)
@@ -124,7 +125,7 @@
 
     def begin(self):
         g = self.g
-        own = self.src.at[self.rows, self.mine]
+        own = self.src.at[pl.ds(self.row, self.rows), self.mine]
         for dz in range(1, g.Z):
             self.push(own, self.view(g.f, self.mine), self.z_base + dz - 1, g.z_peer(dz))
         for dy in range(1, g.Y):
@@ -146,13 +147,8 @@
 
     def over_x(self, dz, dy):
         g = self.g
-        shard = g.source(dz, dy)
-        self.push(
-            self.view(shard, self.x_out),
-            self.view(shard, self.x_out),
-            self.x_base + self.slot(dz, dy),
-            g.x_peer(),
-        )
+        view = self.view(g.source(dz, dy), self.x_out)
+        self.push(view, view, self.x_base + self.slot(dz, dy), g.x_peer())
 
     def finish_y(self):
         g = self.g
@@ -167,12 +163,8 @@
         for dz, dy in self.pairs():
             shard = g.source(dz, dy)
             self.arrive(self.view(shard, self.x_in), self.x_base + self.slot(dz, dy))
-            self.push(
-                self.view(shard, self.core_out),
-                self.view(shard, self.core_out),
-                self.c_base + self.slot(dz, dy),
-                g.core_peer(),
-            )
+            view = self.view(shard, self.core_out)
+            self.push(view, view, self.c_base + self.slot(dz, dy), g.core_peer())
 
     def finish(self):
         g = self.g
@@ -185,71 +177,8 @@
             copy.wait_send()
 
 
-def gather_kernel(grid, pieces, *refs):
-    n = len(pieces)
-    count = refs_count(pieces)
-    sources, outs = refs[:count], refs[count : 2 * count]
-    send, recv, local = refs[2 * count :]
-    grid.locate()
-    owns = []
-    for index in range(count):
-        own = pltpu.make_async_copy(sources[index], outs[index].at[grid.f], local.at[index])
-        own.start()
-        owns.append(own)
-    grid.greet()
-    chunks = [
-        Gather(grid, sources[which], outs[which], pl.ds(row, rows), col, width, send.at[i], recv.at[i])
-        for i, (which, row, rows, col, width) in enumerate(pieces)
-    ]
-    for chunk in chunks:
-        chunk.begin()
-    for step in range(n + 2):
-        if step < n:
-            chunks[step].over_y()
-        if 0 <= step - 1 < n:
-            chunks[step - 1].finish_y()
-        if 0 <= step - 2 < n:
-            chunks[step - 2].over_core()
-    for chunk in chunks:
-        chunk.finish()
-    for chunk in chunks:
-        chunk.drain()
-    for own in owns:
-        own.wait()
-
-
 def refs_count(pieces):
     return 1 + max(piece[0] for piece in pieces)
-
-
-def gather_all(fsdp, dp, arrays):
-    grid = Grid(fsdp, dp)
-    pieces = []
-    for which, array in enumerate(arrays):
-        rows, width = array.shape
-        if rows * width < 96 * 3072 * 96 // fsdp // 12 // 8 * 8 or which < 3:
-            pieces.append((which, 0, rows, 0, width))
-        elif width > 1536:
-            pieces.append((which, 0, rows, 0, width // 2))
-            pieces.append((which, 0, rows, width // 2, width // 2))
-        else:
-            pieces.append((which, 0, rows // 2, 0, width))
-            pieces.append((which, rows // 2, rows // 2, 0, width))
-    count = Gather.count(grid)
-    hbm = pl.BlockSpec(memory_space=pltpu.HBM)
-    return pl.pallas_call(
-        functools.partial(gather_kernel, grid, pieces),
-        out_shape=[jax.ShapeDtypeStruct((fsdp,) + a.shape, a.dtype) for a in arrays],
-        in_specs=[hbm] * len(arrays),
-        out_specs=[hbm] * len(arrays),
-        scratch_shapes=[
-            pltpu.SemaphoreType.DMA((len(pieces), count)),
-            pltpu.SemaphoreType.DMA((len(pieces), count)),
-            pltpu.SemaphoreType.DMA((len(arrays),)),
-        ],
-        compiler_params=pltpu.CompilerParams(collective_id=0, has_side_effects=True),
-        name="gather_weights",
-    )(*arrays)
 
 
 class Scatter:
@@ -486,28 +415,418 @@
 
 
 NORM_EPSILON = 1e-06
-
-
-def layer_norm(values, gain, shift):
-    centred = values - jnp.mean(values, axis=-1, keepdims=True)
-    variance = jnp.mean(centred * centred, axis=-1, keepdims=True)
-    return centred * lax.rsqrt(variance + NORM_EPSILON) * gain + shift
-
-
-def project_rows(left, right):
-    return jnp.einsum("psd,de->pse", left, right, preferred_element_type=jnp.float32)
-
-
-def back_rows(left, right):
-    return jnp.einsum("pse,de->psd", left, right, preferred_element_type=jnp.float32)
-
-
-def outer_rows(left, right):
-    return jnp.einsum("psd,pse->de", left, right, preferred_element_type=jnp.float32)
-
-
-def row_total(values):
-    return jnp.sum(values.astype(jnp.float32), axis=(0, 1))
+PAD = 288
+LOW = jnp.bfloat16
+WIDE = jnp.float32
+SMALL = ("gain_one", "shift_one", "heads", "project", "gain_two", "shift_two", "expand", "shrink")
+
+
+def dot(left, right):
+    return jnp.dot(left, right, preferred_element_type=WIDE)
+
+
+def dot_t(left, right):
+    return lax.dot_general(left, right, (((1,), (1,)), ((), ())), preferred_element_type=WIDE)
+
+
+def t_dot(left, right):
+    return lax.dot_general(left, right, (((0,), (0,)), ((), ())), preferred_element_type=WIDE)
+
+
+def padded_rows(value, length):
+    wide = value.astype(WIDE)
+    if length == PAD:
+        return wide
+    return jnp.concatenate([wide, jnp.zeros((PAD - length, wide.shape[1]), WIDE)], axis=0)
+
+
+def centre(wide):
+    centred = wide - jnp.mean(wide, axis=-1, keepdims=True)
+    scale = lax.rsqrt(jnp.mean(centred * centred, axis=-1, keepdims=True) + NORM_EPSILON)
+    return centred * scale, scale
+
+
+def norm_back(grad, normed, scale, gain):
+    inner = grad * gain
+    return scale * (
+        inner
+        - jnp.mean(inner, axis=-1, keepdims=True)
+        - normed * jnp.mean(inner * normed, axis=-1, keepdims=True)
+    )
+
+
+def gelu_parts(value):
+    bell = jnp.exp(value * value * -0.5)
+    t = 1.0 / (1.0 + jnp.abs(value) * (0.3275911 * 0.7071067811865476))
+    poly = t * (
+        0.5 * 0.254829592
+        + t
+        * (
+            0.5 * -0.284496736
+            + t * (0.5 * 1.421413741 + t * (0.5 * -1.453152027 + t * (0.5 * 1.061405429)))
+        )
+    )
+    tail = poly * bell
+    return jnp.where(value >= 0, 1.0 - tail, tail), value * bell * 0.3989422804014327
+
+
+def unpack_small(fsdp, packed, vectors):
+    first = jnp.zeros((8, 768), WIDE)
+    heads = [jnp.zeros((8, 768), WIDE) for _ in range(2)]
+    hidden = [jnp.zeros((8, 768), WIDE) for _ in range(4)]
+    for f in range(fsdp):
+        rows = packed[pl.ds(8 * f, 8), :].astype(WIDE)
+
+        def turned(length):
+            start = f * length // fsdp
+            return start // 768, (pltpu.roll(rows, start % 768, 1) if start % 768 else rows)
+
+        _, value = turned(768)
+        first += value
+        part, value = turned(1536)
+        heads[part] += value
+        part, value = turned(3072)
+        hidden[part] += value
+    vectors[0:8, :] = first
+    vectors[2:3, :] = heads[0][2:3]
+    vectors[8:9, :] = heads[1][2:3]
+    for part in range(4):
+        vectors[9 + part : 10 + part, :] = hidden[part][6:7]
+
+
+def attend(keep_bias, qkv, context, lse, base, width):
+    first = lax.broadcasted_iota(jnp.int32, (1, 128), 1) < 64
+
+    def heads(step, carry):
+        at = pl.multiple_of(step * 128, 128)
+        rows = pl.ds(base, PAD)
+        query = qkv[rows, pl.ds(at, 128)] * LOW(0.125)
+        key = qkv[rows, pl.ds(at + width, 128)]
+        value = qkv[rows, pl.ds(at + 2 * width, 128)]
+        outs = []
+        for head in range(2):
+            chosen = first if head == 0 else ~first
+            scores = dot_t(jnp.where(chosen, query, LOW(0)), key) + keep_bias
+            top = jnp.max(scores, axis=-1, keepdims=True)
+            expo = jnp.exp(scores - top)
+            total = jnp.sum(expo, axis=-1, keepdims=True)
+            outs.append((dot(expo.astype(LOW), value) * (1.0 / total), top + jnp.log(total)))
+        context[rows, pl.ds(at, 128)] = jnp.where(first, outs[0][0], outs[1][0]).astype(LOW)
+        lse[rows, pl.ds(at, 128)] = jnp.where(first, outs[0][1], outs[1][1])
+        return carry
+
+    return heads
+
+
+def forward_kernel(grid, sizes, counts, *refs):
+    pairs, length, width, hidden = sizes
+    (
+        inputs,
+        cotangent,
+        packed_in,
+        triple_in,
+        project_in,
+        expand_in,
+        shrink_in,
+        layer_out,
+        normed_out,
+        qkv_out,
+        context_out,
+        lse_out,
+        middle_grad_out,
+        context_grad_out,
+        triple_out,
+        vectors_out,
+        sums_out,
+        shrink_grad_out,
+        expand_grad_out,
+        project_grad_out,
+        packed,
+        triple,
+        project,
+        expand,
+        shrink,
+        vectors,
+        sums,
+        normed,
+        qkv,
+        context,
+        lse,
+        normed_two,
+        upstream,
+        branch,
+        activated,
+        pre_grad,
+        stage_out,
+        stage_ctx,
+        send,
+        recv,
+        local,
+        out_sem,
+    ) = refs
+    g = grid.locate()
+    fsdp = grid.F
+    sources = (packed_in, triple_in, project_in, expand_in, shrink_in)
+    wholes = (packed, triple, project, expand, shrink)
+    owns = []
+    for index in range(5):
+        depth = sources[index].shape[0]
+        own = pltpu.make_async_copy(
+            sources[index],
+            wholes[index].at[pl.ds(pl.multiple_of(g.f * depth, 8), depth)],
+            local.at[index],
+        )
+        own.start()
+        owns.append(own)
+    grid.greet()
+    shrink_rows = shrink_in.shape[0]
+    plan = [(0, 0, 8, 0, 768)]
+    plan += [(1, 0, triple_in.shape[0], col, 768) for col in range(0, 3 * width, 768)]
+    plan += [(2, 0, project_in.shape[0], 0, width)]
+    plan += [(3, 0, expand_in.shape[0], col, hidden // 2) for col in (0, hidden // 2)]
+    plan += [(4, row, shrink_rows // 2, 0, width) for row in (0, shrink_rows // 2)]
+    chunks = [
+        Gather(
+            grid,
+            sources[which],
+            wholes[which],
+            sources[which].shape[0],
+            row,
+            rows,
+            col,
+            span,
+            send.at[i],
+            recv.at[i],
+        )
+        for i, (which, row, rows, col, span) in enumerate(plan)
+    ]
+    n = len(chunks)
+    ahead = 4
+
+    def turn(step):
+        if step + ahead < n:
+            chunks[step + ahead].begin()
+        if step < n:
+            chunks[step].over_y()
+        if 0 <= step - 1 < n:
+            chunks[step - 1].finish_y()
+        if 0 <= step - 2 < n:
+            chunks[step - 2].over_core()
+
+    for i in range(ahead):
+        chunks[i].begin()
+    writes = []
+
+    def write(src, dst, index):
+        copy = pltpu.make_async_copy(src, dst, out_sem.at[index])
+        copy.start()
+        writes.append(copy)
+
+    for step in range(3):
+        turn(step)
+    owns[0].wait()
+    chunks[0].finish()
+    unpack_small(fsdp, packed, vectors)
+    sums[...] = jnp.zeros_like(sums)
+    write(vectors, vectors_out, 0)
+
+    def vector(row, rows=1):
+        return vectors[row : row + rows, :]
+
+    def norm_one(b, carry):
+        at = pl.multiple_of(b * PAD, 32)
+        value, _ = centre(padded_rows(inputs[b], length))
+        normed[pl.ds(at, PAD), :] = (value * vector(0) + vector(1)).astype(LOW)
+        return carry
+
+    turn(3)
+    lax.fori_loop(0, pairs, norm_one, 0)
+    write(normed, normed_out, 1)
+    turn(4)
+    turn(5)
+    owns[1].wait()
+    for i in range(1, 4):
+        chunks[i].finish()
+    write(triple, triple_out, 2)
+    left = list(range(6, n + 2))
+    per_pair = -(-len(left) // pairs)
+
+    for b in range(pairs):
+        base = b * PAD
+        rows = pl.ds(base, PAD)
+        for part in range(3):
+            cols = pl.ds(part * width, width)
+            bias = vector(2) if part == 0 else vector(8)
+            value = dot(normed[rows, :], triple[:, cols])
+            qkv[rows, cols] = (value if part == 1 else value + bias).astype(LOW)
+        limit = TEXT + counts[b]
+        keep = lax.broadcasted_iota(jnp.int32, (1, PAD), 1) < limit
+        body = attend(jnp.where(keep, 0.0, -1e30), qkv, context, lse, base, width)
+        lax.fori_loop(0, width // 128, body, 0)
+        for _ in range(per_pair):
+            if left:
+                turn(left.pop(0))
+    write(qkv, qkv_out, 3)
+    write(context, context_out, 4)
+    write(lse, lse_out, 5)
+    for step in left:
+        turn(step)
+    for own in owns[2:]:
+        own.wait()
+    for i in range(4, n):
+        chunks[i].finish()
+
+    for chunk in chunks:
+        chunk.drain()
+    writes[-1].wait()
+    stage_mid, stage_shrink, stage_expand = lse, shrink, expand
+    block = hidden // 3
+
+    def feed(b, carry):
+        at = pl.multiple_of(b * PAD, 32)
+        rows = pl.ds(at, PAD)
+        limit = TEXT + counts[b]
+        valid = lax.broadcasted_iota(jnp.int32, (PAD, 1), 0) < limit
+        middle = padded_rows(inputs[b], length) + dot(context[rows, :], project[...]) + vector(3)
+        value, scale = centre(middle)
+        second = (value * vector(4) + vector(5)).astype(LOW)
+        normed_two[rows, :] = second
+        above = jnp.where(valid, padded_rows(cotangent[b], length), 0.0)
+        above_low = above.astype(LOW)
+        upstream[rows, :] = above_low
+        mixed = jnp.zeros((PAD, width), WIDE)
+        back = jnp.zeros((PAD, width), WIDE)
+        for part in range(3):
+            cols = slice(part * block, (part + 1) * block)
+            bias = jnp.concatenate([vector(9 + i) for i in range(4)], axis=1)[:, cols]
+            pre = dot(second, expand[:, cols]) + bias
+            act_grad = dot_t(above_low, shrink[cols, :])
+            share, slope = gelu_parts(pre)
+            act = (pre * share).astype(LOW)
+            activated[rows, cols] = act
+            grad = (act_grad * (share + slope)).astype(LOW)
+            pre_grad[rows, cols] = grad
+            mixed += dot(act, shrink[cols, :])
+            back += dot_t(grad, expand[:, cols])
+            sums[0:1, cols] += jnp.sum(grad.astype(WIDE), axis=0, keepdims=True)
+        layer = jnp.where(valid, middle + mixed + vector(7), 0.0)
+        stage_out[b] = layer[:length].astype(LOW)
+        middle_grad = above + norm_back(back, value, scale, vector(4))
+        stage_mid[rows, :] = middle_grad
+        low_grad = middle_grad.astype(LOW)
+        branch[rows, :] = low_grad
+        stage_ctx[rows, :] = dot_t(low_grad, project[...]).astype(LOW)
+        for row, term in (
+            (1, above),
+            (2, low_grad.astype(WIDE)),
+            (3, back * value),
+            (4, back),
+        ):
+            sums[row : row + 1, 0:width] += jnp.sum(term, axis=0, keepdims=True)
+        return carry
+
+    lax.fori_loop(0, pairs, feed, 0)
+    write(stage_out, layer_out, 6)
+    write(stage_mid, middle_grad_out, 7)
+    write(stage_ctx, context_grad_out, 8)
+    write(sums, sums_out, 9)
+
+    def shrink_grad(i, carry):
+        at = pl.multiple_of(i * 384, 384)
+        stage_shrink[pl.ds(at, 384), :] = t_dot(
+            activated[:, pl.ds(at, 384)], upstream[...]
+        ).astype(LOW)
+        return carry
+
+    lax.fori_loop(0, hidden // 384, shrink_grad, 0)
+    write(stage_shrink, shrink_grad_out, 10)
+
+    def expand_grad(i, carry):
+        at = pl.multiple_of(i * 256, 256)
+        for part in range(3):
+            cols = slice(part * block, (part + 1) * block)
+            stage_expand[pl.ds(at, 256), cols] = t_dot(
+                normed_two[:, pl.ds(at, 256)], pre_grad[:, cols]
+            ).astype(LOW)
+        return carry
+
+    lax.fori_loop(0, width // 256, expand_grad, 0)
+    write(stage_expand, expand_grad_out, 11)
+    for copy in writes[2:3]:
+        copy.wait()
+    project_stage = triple.at[:, pl.ds(0, width)]
+
+    def project_grad(i, carry):
+        at = pl.multiple_of(i * 256, 256)
+        project_stage[pl.ds(at, 256), :] = t_dot(context[:, pl.ds(at, 256)], branch[...]).astype(LOW)
+        return carry
+
+    lax.fori_loop(0, width // 256, project_grad, 0)
+    write(project_stage, project_grad_out, 12)
+    for i, copy in enumerate(writes):
+        if i not in (2, 5):
+            copy.wait()
+
+
+def run_forward(fsdp, dp, counts, inputs, cotangent, packed, triple, project, expand, shrink):
+    grid = Grid(fsdp, dp)
+    pairs, length, width = inputs.shape
+    hidden = expand.shape[1]
+    rows = pairs * PAD
+    hbm = pl.BlockSpec(memory_space=pltpu.HBM)
+    vmem = pl.BlockSpec(memory_space=pltpu.VMEM)
+    count = Gather.count(grid)
+    shape = jax.ShapeDtypeStruct
+    outs = [
+        shape((pairs, length, width), LOW),
+        shape((rows, width), LOW),
+        shape((rows, 3 * width), LOW),
+        shape((rows, width), LOW),
+        shape((rows, width), WIDE),
+        shape((rows, width), WIDE),
+        shape((rows, width), LOW),
+        shape((width, 3 * width), LOW),
+        shape((16, width), WIDE),
+        shape((8, hidden), WIDE),
+        shape((hidden, width), LOW),
+        shape((width, hidden), LOW),
+        shape((width, width), LOW),
+    ]
+    scratch = [
+        pltpu.VMEM((fsdp * 8, 768), LOW),
+        pltpu.VMEM((width, 3 * width), LOW),
+        pltpu.VMEM((width, width), LOW),
+        pltpu.VMEM((width, hidden), LOW),
+        pltpu.VMEM((hidden, width), LOW),
+        pltpu.VMEM((16, width), WIDE),
+        pltpu.VMEM((8, hidden), WIDE),
+        pltpu.VMEM((rows, width), LOW),
+        pltpu.VMEM((rows, 3 * width), LOW),
+        pltpu.VMEM((rows, width), LOW),
+        pltpu.VMEM((rows, width), WIDE),
+        pltpu.VMEM((rows, width), LOW),
+        pltpu.VMEM((rows, width), LOW),
+        pltpu.VMEM((rows, width), LOW),
+        pltpu.VMEM((rows, hidden), LOW),
+        pltpu.VMEM((rows, hidden), LOW),
+        pltpu.VMEM((pairs, length, width), LOW),
+        pltpu.VMEM((rows, width), LOW),
+        pltpu.SemaphoreType.DMA((9, count)),
+        pltpu.SemaphoreType.DMA((9, count)),
+        pltpu.SemaphoreType.DMA((5,)),
+        pltpu.SemaphoreType.DMA((13,)),
+    ]
+    return pl.pallas_call(
+        functools.partial(forward_kernel, grid, (pairs, length, width, hidden)),
+        out_shape=outs,
+        in_specs=[pl.BlockSpec(memory_space=pltpu.SMEM), vmem, vmem] + [hbm] * 5,
+        out_specs=[hbm] * len(outs),
+        scratch_shapes=scratch,
+        compiler_params=pltpu.CompilerParams(
+            collective_id=0, has_side_effects=True, vmem_limit_bytes=63 * 1024 * 1024
+        ),
+        name="forward_and_feed_back",
+    )(counts, inputs, cotangent, packed, triple, project, expand, shrink)
 
 
 def shards(
@@ -539,141 +858,94 @@
         reduce_bias,
     )
     packed = jnp.stack([jnp.pad(item, (0, 768 - item.shape[0])) for item in small])
-    packed, triple, project, expand, shrink = gather_all(
-        fsdp, dp, (packed, triple_weight, output_weight, expand_weight, reduce_weight)
-    )
-    gain_one, shift_one, biases, project_bias, gain_two, shift_two, expand_add, shrink_add = (
-        packed[:, index, : item.shape[0]].reshape(-1) for index, item in enumerate(small)
-    )
-    triple = triple.reshape(-1, triple.shape[-1])
-    project = project.reshape(-1, project.shape[-1])
-    expand = expand.reshape(-1, expand.shape[-1])
-    shrink = shrink.reshape(-1, shrink.shape[-1])
+    (
+        layer_output,
+        hidden_one,
+        triple_rows,
+        context,
+        lse,
+        middle_grad,
+        context_grad,
+        triple,
+        vectors,
+        sums,
+        shrink_grad,
+        expand_grad,
+        project_grad,
+    ) = run_forward(
+        fsdp,
+        dp,
+        patch_count,
+        inputs,
+        cotangent,
+        packed,
+        triple_weight,
+        output_weight,
+        expand_weight,
+        reduce_weight,
+    )
     pairs, length, width = inputs.shape
+    gain_one = vectors[0]
+
+    def rows(value):
+        return value.reshape(pairs, PAD, -1)[:, :length]
+
+    triple_rows, lse, middle_grad, context_grad, hidden_one = (
+        rows(item) for item in (triple_rows, lse, middle_grad, context_grad, hidden_one)
+    )
+    inputs_wide = inputs.astype(WIDE)
+    query_rows, key_rows, value_rows = (
+        triple_rows[..., i * width : (i + 1) * width].reshape(pairs, length, HEADS, HEAD_DIM)
+        for i in range(3)
+    )
+    context_grad = context_grad.reshape(pairs, length, HEADS, HEAD_DIM)
+    row_lse = lse.reshape(pairs, length, HEADS, HEAD_DIM)[..., 0].transpose(0, 2, 1)[..., None]
     positions = lax.broadcasted_iota(jnp.int32, (pairs, length), 1)
-    valid_rows = (positions < TEXT + patch_count[:, None]).astype(jnp.float32)
-    key_mask = valid_rows[:, None, None, :] > 0
-    score_scale = HEAD_DIM ** (-0.5)
-    inputs_wide = inputs.astype(jnp.float32)
-    hidden_one = layer_norm(
-        inputs_wide, gain_one.astype(jnp.float32), shift_one.astype(jnp.float32)
-    ).astype(jnp.bfloat16)
-    biases_wide = biases.astype(jnp.float32)
-    bias_row = jnp.concatenate(
-        [biases_wide[:width], jnp.zeros((width,), jnp.float32), biases_wide[width:]]
-    )
-    triple_rows = (project_rows(hidden_one, triple) + bias_row).astype(jnp.bfloat16)
-    query_rows = triple_rows[..., :width].reshape(pairs, length, HEADS, HEAD_DIM)
-    key_rows = triple_rows[..., width : 2 * width].reshape(pairs, length, HEADS, HEAD_DIM)
-    value_rows = triple_rows[..., 2 * width :].reshape(pairs, length, HEADS, HEAD_DIM)
-
-    def scores_of(queries_in, keys_in):
-        raw_scores = (
-            jnp.einsum("pshd,pthd->phst", queries_in, keys_in, preferred_element_type=jnp.float32)
-            * score_scale
-        )
-        return jnp.where(key_mask, raw_scores, -1e30)
-
-    scores = scores_of(query_rows, key_rows)
-    row_max = jnp.max(scores, axis=-1, keepdims=True)
-    expo = jnp.exp(scores - row_max)
-    expo_total = jnp.sum(expo, axis=-1, keepdims=True)
-    probs = expo / expo_total
-    row_lse = row_max + jnp.log(expo_total)
-    context = jnp.einsum(
-        "phst,pthd->pshd",
-        probs.astype(jnp.bfloat16),
-        value_rows,
-        preferred_element_type=jnp.float32,
-    )
-    context = context.reshape(pairs, length, width).astype(jnp.bfloat16)
-    middle = inputs_wide + project_rows(context, project) + project_bias.astype(jnp.float32)
-    hidden_two = layer_norm(
-        middle, gain_two.astype(jnp.float32), shift_two.astype(jnp.float32)
-    ).astype(jnp.bfloat16)
-    pre_act = project_rows(hidden_two, expand) + expand_add.astype(jnp.float32)
-    activated = jax.nn.gelu(pre_act, approximate=False).astype(jnp.bfloat16)
-    mixed = project_rows(activated, shrink) + shrink_add.astype(jnp.float32)
-    layer_output = (valid_rows[..., None] * (middle + mixed)).astype(jnp.bfloat16)
-    gain_one_back, triple_back, project_back = gain_one, triple, project
-    gain_two_back, expand_back, shrink_back = gain_two, expand, shrink
-    upstream = cotangent.astype(jnp.float32) * valid_rows[..., None]
-    upstream_low = upstream.astype(jnp.bfloat16)
-    shrink_add_grad = row_total(upstream_low)
-    shrink_grad = outer_rows(activated, upstream_low)
-    act_grad = back_rows(upstream_low, shrink_back)
-    gelu_value, gelu_back = jax.vjp(lambda entry: jax.nn.gelu(entry, approximate=False), pre_act)
-    pre_grad = gelu_back(act_grad)[0].astype(jnp.bfloat16)
-    expand_add_grad = row_total(pre_grad)
-    expand_grad = outer_rows(hidden_two, pre_grad)
-    hidden_two_grad = back_rows(pre_grad, expand_back)
-    zero_shift = jnp.zeros((width,), jnp.float32)
-    norm_value, norm_back_two = jax.vjp(
-        layer_norm, middle, gain_two_back.astype(jnp.float32), zero_shift
-    )
-    middle_part, gain_two_grad, shift_two_grad = norm_back_two(hidden_two_grad)
-    middle_grad = upstream + middle_part
-    branch_low = middle_grad.astype(jnp.bfloat16)
-    project_bias_grad = row_total(branch_low)
-    project_grad = outer_rows(context, branch_low)
-    context_grad = (
-        back_rows(branch_low, project_back)
-        .astype(jnp.bfloat16)
-        .reshape(pairs, length, HEADS, HEAD_DIM)
-    )
-    probs_again = jnp.exp(scores_of(query_rows, key_rows) - row_lse)
+    key_mask = (positions < TEXT + patch_count[:, None])[:, None, None, :]
+    scores = jnp.einsum("pshd,pthd->phst", query_rows, key_rows, preferred_element_type=WIDE) * 0.125
+    probs_again = jnp.exp(jnp.where(key_mask, scores, -1e30) - row_lse)
     value_grad = jnp.einsum(
-        "phst,pshd->pthd",
-        probs_again.astype(jnp.bfloat16),
-        context_grad,
-        preferred_element_type=jnp.float32,
+        "phst,pshd->pthd", probs_again.astype(LOW), context_grad, preferred_element_type=WIDE
     )
     probs_grad = jnp.einsum(
-        "pshd,pthd->phst", context_grad, value_rows, preferred_element_type=jnp.float32
+        "pshd,pthd->phst", context_grad, value_rows, preferred_element_type=WIDE
     )
     score_grad = (
         probs_again * (probs_grad - jnp.sum(probs_again * probs_grad, axis=-1, keepdims=True))
-    ).astype(jnp.bfloat16)
+    ).astype(LOW)
     query_grad = (
-        jnp.einsum("phst,pthd->pshd", score_grad, key_rows, preferred_element_type=jnp.float32)
-        * score_scale
+        jnp.einsum("phst,pthd->pshd", score_grad, key_rows, preferred_element_type=WIDE) * 0.125
     )
     key_grad = (
-        jnp.einsum("phst,pshd->pthd", score_grad, query_rows, preferred_element_type=jnp.float32)
-        * score_scale
+        jnp.einsum("phst,pshd->pthd", score_grad, query_rows, preferred_element_type=WIDE) * 0.125
     )
     triple_grad_rows = jnp.concatenate(
-        [
-            query_grad.reshape(pairs, length, width),
-            key_grad.reshape(pairs, length, width),
-            value_grad.reshape(pairs, length, width),
-        ],
-        axis=-1,
-    ).astype(jnp.bfloat16)
-    bias_sums = row_total(triple_grad_rows)
+        [item.reshape(pairs, length, width) for item in (query_grad, key_grad, value_grad)], axis=-1
+    ).astype(LOW)
+    bias_sums = jnp.sum(triple_grad_rows.astype(WIDE), axis=(0, 1))
     head_bias_grad = jnp.concatenate([bias_sums[:width], bias_sums[2 * width :]])
-    triple_grad = outer_rows(hidden_one, triple_grad_rows)
-    hidden_one_grad = back_rows(triple_grad_rows, triple_back)
-    norm_again, norm_back_one = jax.vjp(
-        layer_norm, inputs_wide, gain_one_back.astype(jnp.float32), zero_shift
-    )
-    input_part, gain_one_grad, shift_one_grad = norm_back_one(hidden_one_grad)
-    input_gradient = (middle_grad + input_part).astype(jnp.bfloat16)
+    triple_grad = jnp.einsum("psd,pse->de", hidden_one, triple_grad_rows, preferred_element_type=WIDE)
+    hidden_one_grad = jnp.einsum(
+        "pse,de->psd", triple_grad_rows, triple, preferred_element_type=WIDE
+    )
+    normed, scale = centre(inputs_wide)
+    gain_one_grad = jnp.sum(hidden_one_grad * normed, axis=(0, 1))
+    shift_one_grad = jnp.sum(hidden_one_grad, axis=(0, 1))
+    input_gradient = (middle_grad + norm_back(hidden_one_grad, normed, scale, gain_one)).astype(LOW)
     small_grads = (
         gain_one_grad,
         shift_one_grad,
         head_bias_grad,
-        project_bias_grad,
-        gain_two_grad,
-        shift_two_grad,
-        expand_add_grad,
-        shrink_add_grad,
+        sums[2, :width],
+        sums[3, :width],
+        sums[4, :width],
+        sums[0],
+        sums[1, :width],
     )
     packed_grad = jnp.stack(
         [
             jnp.pad(
-                item.astype(jnp.bfloat16).reshape(fsdp, -1),
-                ((0, 0), (0, 768 - item.shape[0] // fsdp)),
+                item.astype(LOW).reshape(fsdp, -1), ((0, 0), (0, 768 - item.shape[0] // fsdp))
             )
             for item in small_grads
         ],
@@ -683,7 +955,7 @@
         fsdp,
         dp,
         tuple(
-            item.astype(jnp.bfloat16).reshape(fsdp, -1, item.shape[-1])
+            item.astype(LOW).reshape(fsdp, -1, item.shape[-1])
             for item in (shrink_grad, expand_grad, project_grad, triple_grad)
         )
         + (packed_grad,),

time: 518 us -> 419 us (0.81)
  matrix products: 178 us -> 74.4 us
  Pallas kernels: 177 us -> 248 us
  other arithmetic: 92.8 us -> 27.8 us
    dot_general x15 -> x4, matrix products: 144 us -> 41.1 us  [the longest x1 14 us: shards(): jnp.einsum('phst,pshd->pthd', probs_again.astype(LOW), context_grad, pref...]
    pallas_call x1, Pallas kernels: 78.1 us -> 150 us  [run_forward(): pl.pallas_call(functools.partial(forward_kernel, grid, (pairs, length, wi...]
    convert_element_type x6 -> x1, other arithmetic: 41 us -> 2.17 us  [shards(): (middle_grad + norm_back(hidden_one_grad, normed, scale, gain_one)).astyp...]
    reduce_sum x8 -> x3, other arithmetic: 30 us -> 6.13 us  [the longest x1 2.13 us: shards(): bias_sums = jnp.sum(triple_grad_rows.astype(WIDE), axis=(0, 1))]
    slice x7 -> x12, local copies, waits for them, and re-layouts: 11.9 us -> 22.4 us  [the longest x4 15.8 us: shards(): triple_rows[..., i * width:(i + 1) * width]]
    convert_element_type x11 -> x7, local copies, waits for them, and re-layouts: 9.21 us -> 0.53 us  [shards(): item.astype(LOW).reshape(fsdp, -1)]
    reshape x6 -> x3, local copies, waits for them, and re-layouts: 14.4 us -> 12.5 us  [shards(): item.reshape(pairs, length, width)]
    unnamed x98 -> x40, local copies, waits for them, and re-layouts: 11.8 us -> 11.5 us
where the time goes in v2:
time: 419 us; the launch traced here: 412 us
  Pallas kernels  248 us (59%)
  matrix products  74.4 us (18%)
  local copies, waits for them, and re-layouts  60.3 us (14%)
  other arithmetic  27.8 us (7%)
    pallas_call x1, Pallas kernels, run_forward(): pl.pallas_call(functools.partial(forward_kernel, grid, (pairs, length, wi...  150 us
    pallas_call x1, Pallas kernels, scatter_all(): pl.pallas_call(functools.partial(scatter_kernel, grid, pieces), out_shape...  97.5 us
    convert_element_type x1, other arithmetic, shards(): score_grad = (probs_again * (probs_grad - jnp.sum(probs_again * probs_gra...  19.4 us
    dot_general x1, matrix products, shards(): jnp.einsum('pshd,pthd->phst', context_grad, value_rows, preferred_element...  16.8 us
    slice x4, local copies, waits for them, and re-layouts, shards(): triple_rows[..., i * width:(i + 1) * width]  15.8 us
    dot_general x1, matrix products, shards(): jnp.einsum('phst,pshd->pthd', probs_again.astype(LOW), context_grad, pref...  14 us
    reshape x3, local copies, waits for them, and re-layouts, shards(): item.reshape(pairs, length, width)  12.5 us
    dot_general x1, matrix products, shards(): jnp.einsum('pshd,pthd->phst', query_rows, key_rows, preferred_element_typ...  12.5 us

profile of v2, /device:TPU:1, one launch (start us, length us, event | category | flops | bytes accessed | tf_op | source)
XLA Modules:
  0.0 411.6 jit_solution(9191710286161818062)
XLA Ops:
  0.6 0.7 pad.54
  1.3 0.7 pad.55
  2.0 0.7 pad.56
  2.7 0.7 pad.57
  3.3 0.7 pad.58
  4.0 0.7 pad.59
  4.7 0.7 pad.60
  5.3 0.7 pad.61
  6.0 0.6 stack.62.refs_2_
  6.7 150.2 %forward_and_feed_back.1 = (bf16[4,280,768]{2,1,0:T(8,128)(2,1)}, bf16[1152,768]{1,0:T(8,128)(2,1)}, bf16[1152,2304]{1,0:T(8,128)(2,1)}, bf16[1152,768]{1,0:T(8,...) custom-call(s32[4]{0:T(128)} %counts.1, ...), custom_call_target="tpu_custom_call" | custom-call | tf_op jit(solution)/shard_map/forward_and_feed_back/pallas_call | solution.py:819
  156.8 0.0 copy-start.9
  156.8 1.9 convert_reduce_fusion
  158.8 2.1 fusion.20
  160.9 0.8 slice_reduce_fusion.5
  161.6 0.0 copy-done.9
  161.6 0.1 slice.126
  161.8 2.4 copy.64
  164.2 5.0 %fusion.32 = (bf16[4,280,768]{2,1,0:T(8,128)(2,1)}, bf16[4,280,768]{2,1,0:T(8,128)(2,1)}, bf16[4,280,768]{2,1,0:T(8,128)(2,1)}) fusion(bf16[4,288,2304]{2,1,0:T(8,128)(2,1)} %bitcast.82), kind=kLoop, calls=%fused_computation.67 | loop fusion | bytes 10321920 | tf_op jit(solution)/shard_map/slice | solution.py:898
  169.1 2.8 copy.60
  172.0 4.0 copy.59
  176.0 12.5 %fusion.34 = f32[4,12,280,280]{2,3,1,0:T(8,128)} fusion(bf16[4,280,12,64]{1,3,2,0:T(8,128)(2,1)S(1)} %bitcast.73, bf16[4,280,12,64]{1,3,2,0:T(8,128)(2,1)} %bitcast.75), kind=kOutput, calls=%fused_computation.69 | convolution fusion | flops 481689600 | bytes 18493440 | tf_op jit(solution)/shard_map/pshd,pthd->phst/dot_general | solution.py:905
  188.5 0.0 copy-done.7
  188.5 2.1 slice.124
  190.6 5.7 %copy.83 = f32[4,280,768]{1,2,0:T(8,128)} copy(f32[4,280,768]{2,1,0:T(8,128)} %slice.124) | data formatting | bytes 6881280
  196.2 1.1 slice.125
  197.4 0.1 iota_compare_fusion.1
  197.5 14.0 %fusion.21 = bf16[4,12,64,280]{3,2,1,0:T(8,128)(2,1)} fusion(bf16[4,280,12,64]{1,3,2,0:T(8,128)(2,1)} %bitcast.78, f32[4,12,280,280]{2,3,1,0:T(8,128)} %fusion.34, f32[4,12,280]{2,1,0:T(8,128)S(1)} %copy.63, pred[4,280]{1,0:T(4,128)(4,1)S(1)} %iota_compare_fusion.1), kind=kOutput, calls=%fused_computation.30 | convolution fusion | flops 497602560 | bytes 18548320 | tf_op jit(solution)/shard_map/phst,pshd->pthd/dot_general | solution.py:907
  211.4 4.0 copy.71
  215.5 4.0 copy.65
  219.5 16.8 %multiply_reduce_fusion = (f32[4,12,280]{2,1,0:T(8,128)S(1)}, f32[4,12,280,280]{2,3,1,0:T(8,128)}) fusion(f32[4,12,280,280]{2,3,1,0:T(8,128)} %fusion.34, f32[4,12,280]{2,1,0:T(8,128)S(1)} %copy.63, pred[4,280]{1,0:T(4,128)(4,1)S(1)} %iota_compare_fusion.1, bf16[4,280,12,64]{1,3,2,0:T(8,128)(2,1)} %bitcast.79, bf16[4,280,12,64]{1,3,2,0:T(8,128)(2,1)} %bitcast.80), kind=kOutput, calls=%fused_computation.1 | convolution fusion | flops 500492160 | bytes 33654880 | tf_op jit(solution)/shard_map/pshd,pthd->phst/dot_general | solution.py:910
  236.3 19.4 %multiply_convert_fusion = bf16[4,12,280,280]{2,3,1,0:T(8,128)(2,1)} fusion(f32[4,12,280,280]{2,3,1,0:T(8,128)} %get-tuple-element.68, f32[4,12,280,280]{2,3,1,0:T(8,128)} %fusion.34, f32[4,12,280]{2,1,0:T(8,128)S(1)} %get-tuple-element.67, f32[4,12,280]{2,1,0:T(8,128)S(1)} %copy.63, pred[4,280]{1,0:T(4,128)(4,1)S(1)} %iota_compare_fusion.1), kind=kLoop, calls=%fused_computation | loop fusion | flops 22579200 | bytes 37740640 | tf_op jit(solution)/shard_map/convert_element_type | solution.py:915
  255.7 8.8 %multiply_convert_fusion.1 = bf16[4,12,64,280]{3,2,1,0:T(8,128)(2,1)} fusion(bf16[4,280,12,64]{1,3,2,0:T(8,128)(2,1)S(1)} %bitcast.74, bf16[4,12,280,280]{2,3,1,0:T(8,128)(2,1)} %multiply_convert_fusion), kind=kOutput, calls=%fused_computation.11 | convolution fusion | flops 483409920 | bytes 10967040 | tf_op jit(solution)/shard_map/phst,pshd->pthd/dot_general | solution.py:920
  264.5 4.2 %copy.70 = bf16[4,280,768]{2,1,0:T(8,128)(2,1)} copy(bf16[4,280,768]{1,2,0:T(8,128)(2,1)} %bitcast.77) | data formatting | bytes 3440640 | tf_op jit(solution)/shard_map/reshape | solution.py:923
  268.8 7.7 %multiply_convert_fusion.2 = bf16[4,12,64,280]{3,2,1,0:T(8,128)(2,1)} fusion(bf16[4,280,12,64]{1,3,2,0:T(8,128)(2,1)S(1)} %bitcast.76, bf16[4,12,280,280]{2,3,1,0:T(8,128)(2,1)} %multiply_convert_fusion), kind=kOutput, calls=%fused_computation.12 | convolution fusion | flops 483409920 | bytes 10967040 | tf_op jit(solution)/shard_map/phst,pthd->pshd/dot_general | solution.py:917
  276.5 4.3 %copy.69 = bf16[4,280,768]{2,1,0:T(8,128)(2,1)} copy(bf16[4,280,768]{1,2,0:T(8,128)(2,1)} %bitcast.81) | data formatting | bytes 3440640 | tf_op jit(solution)/shard_map/reshape | solution.py:923
  280.7 0.0 copy-done.2
  280.7 7.9 %fusion.19 = (bf16[768]{0:T(1024)(128)(2,1)S(1)}, f32[4,280]{1,0:T(4,128)S(1)}, f32[4,280]{1,0:T(4,128)S(1)}, bf16[768]{0:T(1024)(128)(2,1)S(1)}, f32[4,280,768]{2,1,0:T(8,128)S(1)}) fusion(bf16[4,280,768]{2,1,0:T(8,128)(2,1)S(1)} %copy-done, f32[4,280]{1,0:T(4,128)S(1)} %add_rsqrt_fusion, f32[4,280]{1,0:T(4,128)S(1)} %broadcast_multiply_fusion.2, ...), kind=kOutput, calls=%fused_computation.27 | convolution fusion | flops 3987698176 | bytes 13884928 | tf_op jit(solution)/shard_map/pse,de->psd/dot_general | solution.py:928
  288.7 2.2 fusion.18
  290.9 0.0 copy-done.3
  290.9 0.2 copy-done.5
  291.1 0.8 copy-done.16
  291.8 6.8 %bitcast_convert_fusion = bf16[768,2304]{1,0:T(8,128)(2,1)} fusion(bf16[4,288,768]{2,1,0:T(8,128)(2,1)S(1)} %bitcast.94, bf16[4,280,768]{2,1,0:T(8,128)(2,1)S(1)} %copy-done.2, bf16[4,280,768]{2,1,0:T(8,128)(2,1)S(1)} %copy-done.3, bf16[4,280,768]{2,1,0:T(8,128)(2,1)S(1)} %copy-done.5), kind=kOutput, calls=%fused_computation.9 | convolution fusion | flops 3980869632 | bytes 10420224 | tf_op jit(solution)/shard_map/psd,pse->de/dot_general | solution.py:927
  298.6 0.1 convert_element_type.88
  298.7 0.6 copy.72
  299.3 0.1 convert_element_type.90
  299.4 0.6 copy.73
  300.1 2.1 fusion.31
  302.2 0.1 concatenate.15
  302.3 0.1 concatenate.14
  302.5 0.1 convert_element_type.92
  302.6 0.1 convert_element_type.93
  302.7 0.1 convert_element_type.94
  303.0 0.1 convert_element_type.96
  303.1 1.7 stack.71.refs_4_
  304.8 97.5 %scatter_gradients.1 = (f32[384,768]{1,0:T(8,128)}, f32[96,3072]{1,0:T(8,128)}, f32[96,768]{1,0:T(8,128)}, f32[96,2304]{1,0:T(8,128)}, f32[8,768]{1,0:T(8,128)}) custom-call(bf16[8,384,768]{2,1,0:T(8,128)(2,1)} %bitcast.84, bf16[8,96,3072]{2,1,0:T(8,128)(2,1)} %bitcast.85, bf16[8,96,768]{2,1,0:T(8,128)(2,1)} %bitcast.91, bf16[8,96,2304]{2,1,0:T(8,128)(2,1)} %bitcast.86, ...), custom_call_target="tpu_custom_call" | custom-call | tf_op jit(solution)/shard_map/scatter_gradients/pallas_call | solution.py:399
  402.3 1.4 slice_bitcast_fusion
  403.7 1.3 slice.115
  405.0 1.3 slice_reduce_fusion.6
  406.3 1.2 copy.91
  407.5 0.9 copy.92
  408.4 0.7 copy.93
  409.1 1.0 copy.94
  410.1 0.0 copy-done.10
  410.1 1.0 copy.95
  (59 shorter events, 0.5 us)
Async XLA Ops:
  156.8 4.8 %copy-start.9 = (bf16[1152,768]{1,0:T(8,128)(2,1)S(1)}, bf16[1152,768]{1,0:T(8,128)(2,1)}, u32[]{:S(2)}) copy-start(bf16[1152,768]{1,0:T(8,128)(2,1)} %get-tuple-element.35) | copy-start | bytes 5308420
  176.0 12.5 %copy-start.7 = (f32[1152,768]{1,0:T(8,128)S(1)}, f32[1152,768]{1,0:T(8,128)}, u32[]{:S(2)}) copy-start(f32[1152,768]{1,0:T(8,128)} %get-tuple-element.34) | copy-start | bytes 10616836
  190.6 6.8 %copy-start.15 = (s32[4]{0:T(128)S(1)}, s32[4]{0:T(128)}, u32[]{:S(2)}) copy-start(s32[4]{0:T(128)} %counts.1) | copy-start | bytes 52
  264.5 4.2 %copy-start.1 = (bf16[4,280,768]{1,2,0:T(8,128)(2,1)S(1)}, bf16[4,280,768]{1,2,0:T(8,128)(2,1)}, u32[]{:S(2)}) copy-start(bf16[4,280,768]{1,2,0:T(8,128)(2,1)} %copy.59) | copy-start | bytes 5160964
  276.5 4.3 %copy-start = (bf16[4,280,768]{2,1,0:T(8,128)(2,1)S(1)}, bf16[4,280,768]{2,1,0:T(8,128)(2,1)}, u32[]{:S(2)}) copy-start(bf16[4,280,768]{2,1,0:T(8,128)(2,1)} %refs_0_.1) | copy-start | bytes 5160964
  276.5 4.3 %copy-start.2 = (bf16[4,280,768]{2,1,0:T(8,128)(2,1)S(1)}, bf16[4,280,768]{2,1,0:T(8,128)(2,1)}, u32[]{:S(2)}) copy-start(bf16[4,280,768]{2,1,0:T(8,128)(2,1)} %copy.71) | copy-start | bytes 5160964
  280.7 8.0 %copy-start.6 = (f32[1152,768]{1,0:T(8,128)S(1)}, f32[1152,768]{1,0:T(8,128)}, u32[]{:S(2)}) copy-start(f32[1152,768]{1,0:T(8,128)} %get-tuple-element.32) | copy-start | bytes 10616836
  288.7 2.2 copy-start.3
  288.7 2.4 copy-start.5
  288.7 3.1 copy-start.16
  291.8 8.2 %copy-start.4 = (bf16[4,280,768]{2,1,0:T(8,128)(2,1)S(1)}, bf16[4,280,768]{2,1,0:T(8,128)(2,1)}, u32[]{:S(2)}) copy-start(bf16[4,280,768]{2,1,0:T(8,128)(2,1)} %copy.70) | copy-start | bytes 5160964
  298.6 3.8 copy-start.14
  304.8 101.5 %copy-start.8 = (bf16[4,280,768]{2,1,0:T(8,128)(2,1)S(1)}, bf16[4,280,768]{2,1,0:T(8,128)(2,1)}, u32[]{:S(2)}) copy-start(bf16[4,280,768]{2,1,0:T(8,128)(2,1)} %get-tuple-element.86) | copy-start | bytes 5160964
  402.3 5.2 %copy-start.12 = (f32[96,2304]{1,0:T(8,128)S(1)}, f32[96,2304]{1,0:T(8,128)}, u32[]{:S(2)}) copy-start(f32[96,2304]{1,0:T(8,128)} %get-tuple-element.90) | copy-start | bytes 2654212
  402.3 6.1 %copy-start.13 = (f32[96,768]{1,0:T(8,128)S(1)}, f32[96,768]{1,0:T(8,128)}, u32[]{:S(2)}) copy-start(f32[96,768]{1,0:T(8,128)} %get-tuple-element.92) | copy-start | bytes 884740
  402.3 6.8 %copy-start.11 = (f32[96,3072]{1,0:T(8,128)S(1)}, f32[96,3072]{1,0:T(8,128)}, u32[]{:S(2)}) copy-start(f32[96,3072]{1,0:T(8,128)} %get-tuple-element.96) | copy-start | bytes 3538948
  406.3 3.8 copy-start.10
